TPU v7x, 32 devices: a whole 2x2x4 slice. The times are simulated.
32 devices in a mesh: dp: 8 (over z, y), tensor: 4 (over x, core).
Axes of the slice: x: 2, y: 2, z: 4, core: 2. Of those that a mesh axis runs over, the one named last changes fastest.
Arguments:
- hidden_in: bfloat16 [16384, 768], P(('dp', 'tensor')), may hold values from -6 to 6
- earlier: bfloat16 [4, 16384, 768], P(None, ('dp', 'tensor')), may hold values from -6 to 6
- gain_attn: float32 [768], replicated, may hold values from 0.1 to 1.9
- gain_mlp: float32 [768], replicated, may hold values from 0.1 to 1.9
- w_qkv: bfloat16 [768, 3, 768], P('dp', None, 'tensor'), may hold values from -0.21875 to 0.21875
- w_out: bfloat16 [768, 768], P('tensor', 'dp'), may hold values from -1.75 to 1.75
- w_up: bfloat16 [768, 3072], P('dp', 'tensor'), may hold values from -0.21875 to 0.21875
- w_down: bfloat16 [3072, 768], P('tensor', 'dp'), may hold values from -0.109375 to 0.109375
- mix_weights: float32 [5], replicated, may hold values from 0.3 to 1.2
- lengths: int32 [16, 4], P('dp'), may hold values from 0 to 1024, as said below
- slot_perm: int32 [16384], P('dp'), may hold values from 0 to 2047, as said below
- grad_out: bfloat16 [16384, 768], P(('dp', 'tensor')), may hold values from -6 to 6
Outputs:
- mixed_out: bfloat16 [16384, 768], P(('dp', 'tensor'))
- grad_hidden: bfloat16 [16384, 768], P(('dp', 'tensor'))
- grad_earlier: bfloat16 [4, 16384, 768], P(None, ('dp', 'tensor'))
- grad_gain_attn: float32 [768], replicated
- grad_gain_mlp: float32 [768], replicated
- grad_w_qkv: float32 [768, 3, 768], P('dp', None, 'tensor')
- grad_w_out: float32 [768, 768], P('tensor', 'dp')
- grad_w_up: float32 [768, 3072], P('dp', 'tensor')
- grad_w_down: float32 [3072, 768], P('tensor', 'dp')
- grad_mix: float32 [5], replicated
Inputs may be any that keep to these rules, and one draw needn't show every extreme that they name: Each slot's lengths sum to at most 1024; in every draw some slot holds one sequence of exactly 1024 and entries of 0 there. `slot_perm`: each aligned block of 2048 entries holds every number of 0 to 2047 once.
All inputs are finite; a program needn't handle non-finite values.
Results may differ from a plain program's by a relative error of at most 0.013.
The roundings to bfloat16 on the way count: a program that leaves them out, or rounds other values in their place, can miss the bound.
Values may be sent and summed in bfloat16 or wider, within the bound.
No kernel may reach another device: no remote copies, remote signals or barrier semaphores. Data moves between devices by JAX's collectives and lax.ppermute only.
A program may use at most 192 MiB of HBM per device.

v0:
```python
import jax
import jax.numpy as jnp
from jax import lax
from jax.experimental import pallas as pl
from jax.experimental.pallas import tpu as pltpu
from jax.sharding import PartitionSpec as P


TENSOR = "tensor"
DP = "dp"
HEAD_SIZE = 64
HALF = HEAD_SIZE // 2
LANES = 128
LOG2E = 1.4426950408889634
ROW_STEP = 256

eps = 1e-05
bf16 = jnp.bfloat16
f32 = jnp.float32


def layer_norm(value, gain):
    row_mean = jnp.mean(value, axis=-1, keepdims=True)
    centered = value - row_mean
    spread = jnp.mean(centered * centered, axis=-1, keepdims=True)
    return centered * lax.rsqrt(spread + eps) * gain


def slot_layout(lengths, slot_len):
    ends = jnp.cumsum(lengths, axis=-1)
    places = jnp.arange(slot_len, dtype=jnp.int32)
    passed = places[None, :, None] >= ends[:, None, :]
    first = jnp.max(jnp.where(passed, ends[:, None, :], 0), axis=-1)
    return (first, places[None, :] - first)


def angle_tables(position):
    inverse = 1.0 / 10000.0 ** (jnp.arange(HALF, dtype=f32) * (2.0 / HEAD_SIZE))
    phase_angle = position.astype(f32)[:, None] * inverse[None, :]
    cosine = jnp.cos(phase_angle)
    sine = jnp.sin(phase_angle)
    repeat = LANES // HEAD_SIZE
    return (
        jnp.concatenate([cosine, cosine] * repeat, axis=1),
        jnp.concatenate([-sine, sine] * repeat, axis=1),
    )


def swap_halves(value):
    lane = lax.broadcasted_iota(jnp.int32, value.shape, 1)
    low = (lane % HEAD_SIZE) < HALF
    return jnp.where(low, pltpu.roll(value, LANES - HALF, 1), pltpu.roll(value, HALF, 1))


def turn(value, cosine, sine):
    return value * cosine + swap_halves(value) * sine


def dot(a, b, dims=((1,), (0,))):
    return lax.dot_general(a, b, (dims, ((), ())), preferred_element_type=f32)


def order_kernel(n0, n1, n2, n3, perm_ref, slot_ref):
    slot_ref[...] = pick_rows(perm_ref[...], (n0, n1, n2, n3)).astype(bf16)


def pick_rows(wanted, pieces):
    each = pieces[0].shape[0]
    total = None
    for k in range(4):
        here = lax.broadcasted_iota(jnp.int32, (wanted.shape[0], each), 1) + k * each
        pick = jnp.where(here == wanted, 1.0, 0.0).astype(bf16)
        part = dot(pick, pieces[k][...])
        total = part if total is None else total + part
    return total


def to_slots(pieces, perm_col):
    each, width = pieces[0].shape
    rows = perm_col.shape[0]
    whole = pl.BlockSpec((each, width), lambda i: (0, 0))
    return pl.pallas_call(
        order_kernel,
        grid=(rows // ROW_STEP,),
        in_specs=[whole] * 4 + [pl.BlockSpec((ROW_STEP, 1), lambda i: (i, 0))],
        out_specs=pl.BlockSpec((ROW_STEP, width), lambda i: (i, 0)),
        out_shape=jax.ShapeDtypeStruct((rows, width), bf16),
        name="order",
    )(*pieces, perm_col)


def project_kernel(normed_ref, w_ref, cos_ref, sin_ref, qkv_ref):
    normed = normed_ref[...]
    cosine = cos_ref[...]
    sine = sin_ref[...]
    third = w_ref.shape[2]
    both = jnp.concatenate([dot(normed, w_ref[0]), dot(normed, w_ref[1])], axis=1)
    for start in range(0, 2 * third, LANES):
        qkv_ref[:, start : start + LANES] = turn(
            both[:, start : start + LANES], cosine, sine
        ).astype(bf16)
    qkv_ref[:, 2 * third :] = dot(normed, w_ref[2]).astype(bf16)


def project(normed, w, cosine, sine):
    rows, width = normed.shape
    cols = 3 * w.shape[2]
    step = 2 * ROW_STEP
    return pl.pallas_call(
        project_kernel,
        grid=(rows // step,),
        in_specs=[
            pl.BlockSpec((step, width), lambda i: (i, 0)),
            pl.BlockSpec((3,) + w.shape[1:], lambda i: (0, 0, 0)),
            pl.BlockSpec((step, LANES), lambda i: (i, 0)),
            pl.BlockSpec((step, LANES), lambda i: (i, 0)),
        ],
        out_specs=pl.BlockSpec((step, cols), lambda i: (i, 0)),
        out_shape=jax.ShapeDtypeStruct((rows, cols), bf16),
        name="proj",
    )(normed, w, cosine, sine)


def norm_back(value, gain, grad):
    row_mean = jnp.mean(value, axis=-1, keepdims=True)
    centered = value - row_mean
    spread = jnp.mean(centered * centered, axis=-1, keepdims=True)
    rstd = lax.rsqrt(spread + eps)
    normed = centered * rstd
    scaled = grad * gain
    mean_scaled = jnp.mean(scaled, axis=-1, keepdims=True)
    mean_both = jnp.mean(scaled * normed, axis=-1, keepdims=True)
    return rstd * (scaled - mean_scaled - normed * mean_both), grad * normed


def added(a_ref, b_ref, c_ref):
    return a_ref[...].astype(f32) + b_ref[...].astype(f32) + c_ref[...].astype(f32)


def mid_back_kernel(
    mix_ref, value_ref, gain_ref, a_ref, b_ref, c_ref, grad_ref, *refs
):
    weights, (g_ref, low_ref, gain_out, term_out), outs = refs[:4], refs[4:8], refs[8:]
    back, terms = norm_back(value_ref[...], gain_ref[...], added(a_ref, b_ref, c_ref))
    grad = grad_ref[...].astype(f32)
    total = mix_ref[4] * grad + back
    term_out[0] = jnp.sum(grad * value_ref[...], axis=0, keepdims=True)
    low = total.astype(bf16)
    g_ref[...] = total
    low_ref[...] = low
    gain_out[0] = jnp.sum(terms, axis=0, keepdims=True)
    for w_ref, ref in zip(weights, outs):
        ref[...] = dot(low, w_ref[...]).astype(bf16)


def mid_back(mix, value, gain, grads, cotangent, weights):
    rows, width = value.shape
    cols = weights[0].shape[1]
    steps = rows // ROW_STEP
    block = pl.BlockSpec((ROW_STEP, width), lambda i: (i, 0))
    return pl.pallas_call(
        mid_back_kernel,
        grid=(steps,),
        in_specs=[
            pl.BlockSpec(memory_space=pltpu.SMEM),
            block,
            pl.BlockSpec((1, width), lambda i: (0, 0)),
            block,
            block,
            block,
            block,
        ]
        + [pl.BlockSpec((width, cols), lambda i: (0, 0))] * 4,
        out_specs=[block, block] + [pl.BlockSpec((1, 1, width), lambda i: (i, 0, 0))] * 2
        + [pl.BlockSpec((ROW_STEP, cols), lambda i: (i, 0))] * 4,
        out_shape=[
            jax.ShapeDtypeStruct((rows, width), f32),
            jax.ShapeDtypeStruct((rows, width), bf16),
            jax.ShapeDtypeStruct((steps, 1, width), f32),
            jax.ShapeDtypeStruct((steps, 1, width), f32),
        ]
        + [jax.ShapeDtypeStruct((rows, cols), bf16)] * 4,
        name="mid_b",
    )(mix, value, gain[None], *grads, cotangent, *weights)


def last_back_kernel(value_ref, gain_ref, a_ref, b_ref, c_ref, carry_ref, out_ref):
    back, _ = norm_back(value_ref[...].astype(f32), gain_ref[...], added(a_ref, b_ref, c_ref))
    out_ref[...] = (carry_ref[...] + back).astype(bf16)


def last_back(value, gain, grads, carry):
    rows, width = value.shape
    block = pl.BlockSpec((ROW_STEP, width), lambda i: (i, 0))
    return pl.pallas_call(
        last_back_kernel,
        grid=(rows // ROW_STEP,),
        in_specs=[block, pl.BlockSpec((1, width), lambda i: (0, 0))] + [block] * 4,
        out_specs=block,
        out_shape=jax.ShapeDtypeStruct((rows, width), bf16),
        name="last_b",
    )(value, gain[None], *grads, carry)


def after_attn_kernel(value_ref, gain_ref, *refs):
    heads, weights, (total_ref, normed_ref) = refs[:4], refs[4:8], refs[8:]
    total = value_ref[...].astype(f32)
    for head_ref, w_ref in zip(heads, weights):
        total += dot(head_ref[...], w_ref[...], ((1,), (1,)))
    total_ref[...] = total
    normed_ref[...] = layer_norm(total, gain_ref[...]).astype(bf16)


def project_out(value, gain, heads, weights):
    rows, width = value.shape
    cols = heads[0].shape[1]
    block = pl.BlockSpec((ROW_STEP, width), lambda i: (i, 0))
    return pl.pallas_call(
        after_attn_kernel,
        grid=(rows // ROW_STEP,),
        in_specs=[block, pl.BlockSpec((1, width), lambda i: (0, 0))]
        + [pl.BlockSpec((ROW_STEP, cols), lambda i: (i, 0))] * 4
        + [pl.BlockSpec((width, cols), lambda i: (0, 0))] * 4,
        out_specs=[block, block],
        out_shape=[
            jax.ShapeDtypeStruct((rows, width), f32),
            jax.ShapeDtypeStruct((rows, width), bf16),
        ],
        name="proj_o",
    )(value, gain[None], *heads, *weights)


def mix_early_kernel(mix_ref, earlier_ref, grad_ref, out_ref, prior_ref, terms_ref):
    grad = grad_ref[...].astype(f32)
    prior = None
    for j in range(4):
        value = earlier_ref[j].astype(f32)
        out_ref[j] = (mix_ref[j] * grad).astype(bf16)
        terms_ref[0, j : j + 1, :] = jnp.sum(grad * value, axis=0, keepdims=True)
        part = mix_ref[j] * value
        prior = part if prior is None else prior + part
    prior_ref[...] = prior


def mix_early(mix, earlier, grad):
    rows, width = grad.shape
    steps = rows // ROW_STEP
    block = pl.BlockSpec((ROW_STEP, width), lambda i: (i, 0))
    layers = pl.BlockSpec((4, ROW_STEP, width), lambda i: (0, i, 0))
    return pl.pallas_call(
        mix_early_kernel,
        grid=(steps,),
        in_specs=[pl.BlockSpec(memory_space=pltpu.SMEM), layers, block],
        out_specs=[layers, block, pl.BlockSpec((1, 4, width), lambda i: (i, 0, 0))],
        out_shape=[
            jax.ShapeDtypeStruct(earlier.shape, bf16),
            jax.ShapeDtypeStruct((rows, width), f32),
            jax.ShapeDtypeStruct((steps, 4, width), f32),
        ],
        name="mix_e",
    )(mix, earlier, grad)


def mix_late_kernel(mix_ref, value_ref, a_ref, b_ref, c_ref, prior_ref, out_ref):
    block_out = value_ref[...] + added(a_ref, b_ref, c_ref)
    out_ref[...] = (prior_ref[...] + mix_ref[4] * block_out).astype(bf16)


def mix_late(mix, value, terms, prior):
    rows, width = value.shape
    block = pl.BlockSpec((ROW_STEP, width), lambda i: (i, 0))
    return pl.pallas_call(
        mix_late_kernel,
        grid=(rows // ROW_STEP,),
        in_specs=[pl.BlockSpec(memory_space=pltpu.SMEM)] + [block] * 5,
        out_specs=block,
        out_shape=jax.ShapeDtypeStruct((rows, width), bf16),
        name="mix_l",
    )(mix, value, *terms, prior)


def mlp_kernel(a_ref, b_ref, ga_ref, gb_ref, up_ref, down_ref, *outs):
    c = 0.7978845608028654
    for n, (rows_ref, grad_ref) in enumerate(((a_ref, ga_ref), (b_ref, gb_ref))):
        dn_ref, hid_ref, du_ref = outs[3 * n : 3 * n + 3]
        u = dot(rows_ref[...], up_ref[...])
        square = u * u
        t = jnp.tanh(c * (u * (1.0 + 0.044715 * square)))
        half = 0.5 * (1.0 + t)
        hid_ref[...] = (u * half).astype(bf16)
        slope = half + 0.5 * u * (1.0 - t * t) * (c * (1.0 + 3 * 0.044715 * square))
        du = (dot(grad_ref[...], down_ref[...]) * slope).astype(bf16)
        du_ref[...] = du
        dn_ref[...] = dot(du, up_ref[...], ((1,), (1,))).astype(bf16)


def mlp(rows, grads, updown):
    each, width = rows[0].shape
    units = updown.shape[1] // 2
    block = pl.BlockSpec((ROW_STEP, width), lambda i: (i, 0))
    inner = pl.BlockSpec((ROW_STEP, units), lambda i: (i, 0))
    wide = jax.ShapeDtypeStruct((each, width), bf16)
    mid = jax.ShapeDtypeStruct((each, units), bf16)
    return pl.pallas_call(
        mlp_kernel,
        grid=(each // ROW_STEP,),
        in_specs=[block] * 4
        + [
            pl.BlockSpec((width, units), lambda i: (0, 0)),
            pl.BlockSpec((width, units), lambda i: (0, 1)),
        ],
        out_specs=[block, inner, inner] * 2,
        out_shape=[wide, mid, mid] * 2,
    )(*rows, *grads, updown, updown)


def mlp_out_kernel(h0, h1, h2, h3, down_ref, o0, o1, o2, o3):
    for hid_ref, out_ref in ((h3, o3), (h2, o2), (h1, o1), (h0, o0)):
        out_ref[...] = dot(hid_ref[...], down_ref[...], ((1,), (1,))).astype(bf16)


def mlp_out(hids, updown):
    each, units = hids[0].shape
    width = updown.shape[0]
    return pl.pallas_call(
        mlp_out_kernel,
        grid=(each // ROW_STEP,),
        in_specs=[pl.BlockSpec((ROW_STEP, units), lambda i: (i, 0))] * 4
        + [pl.BlockSpec((width, units), lambda i: (0, 1))],
        out_specs=[pl.BlockSpec((ROW_STEP, width), lambda i: (i, 0))] * 4,
        out_shape=[jax.ShapeDtypeStruct((each, width), bf16)] * 4,
        name="mlp_out",
    )(*hids, updown)


def mlp_weights_kernel(*refs):
    rows, grads, hids, dus = refs[:4], refs[4:8], refs[8:12], refs[12:16]
    down_ref, out_ref, term_ref, acc = refs[16:]
    units = hids[0].shape[1]
    step = pl.program_id(0)

    @pl.when(step == 0)
    def _():
        acc[...] = jnp.zeros(acc.shape, f32)

    up = down = None
    for k in range(4):
        a = dot(rows[k][...], dus[k][...], ((0,), (0,)))
        b = dot(grads[k][...], hids[k][...], ((0,), (0,)))
        up = a if up is None else up + a
        down = b if down is None else down + b
    acc[:, :units] += up
    acc[:, units:] += down

    @pl.when(step == pl.num_programs(0) - 1)
    def _():
        out_ref[...] = acc[...].astype(bf16)
        term_ref[...] = jnp.sum(acc[:, units:] * down_ref[...].astype(f32), axis=0, keepdims=True)


def mlp_weights(rows, grads, hids, dus, updown):
    each, width = rows[0].shape
    units = hids[0].shape[1]
    block = pl.BlockSpec((ROW_STEP, width), lambda i: (i, 0))
    inner = pl.BlockSpec((ROW_STEP, units), lambda i: (i, 0))
    return pl.pallas_call(
        mlp_weights_kernel,
        grid=(each // ROW_STEP,),
        in_specs=[block] * 8 + [inner] * 8 + [pl.BlockSpec((width, units), lambda i: (0, 1))],
        out_specs=[
            pl.BlockSpec((width, 2 * units), lambda i: (0, 0)),
            pl.BlockSpec((1, units), lambda i: (0, 0)),
        ],
        out_shape=[
            jax.ShapeDtypeStruct((width, 2 * units), bf16),
            jax.ShapeDtypeStruct((1, units), f32),
        ],
        scratch_shapes=[pltpu.VMEM((width, 2 * units), f32)],
        name="wmlp",
    )(*rows, *grads, *hids, *dus, updown)


def spread_rows(perm_ref, value, start, count):
    total = value.shape[0]
    here = lax.broadcasted_iota(jnp.int32, (count, total), 0) + start
    pick = jnp.where(here == perm_ref[...], 1.0, 0.0).astype(bf16)
    return dot(pick, value)


def masked(scores, first_row, query_start):
    key = lax.broadcasted_iota(jnp.int32, scores.shape, 0)
    query = lax.broadcasted_iota(jnp.int32, scores.shape, 1) + query_start
    return jnp.where((key >= first_row) & (key <= query), scores, -1e30)


def attend_kernel(qkv_ref, first_ref, perm_ref, o0, o1, o2, o3, stat_ref, o_all):
    slot = pl.program_id(0)
    length, cols = qkv_ref.shape
    third = cols // 3
    factor = HEAD_SIZE ** (-0.5) * LOG2E
    for head in range(third // HEAD_SIZE):
        at = head * HEAD_SIZE
        key = qkv_ref[:, third + at : third + at + HEAD_SIZE]
        value = qkv_ref[:, 2 * third + at : 2 * third + at + HEAD_SIZE]
        value_t = value.T
        for start in range(0, length, ROW_STEP):
            seen = start + ROW_STEP
            query = qkv_ref[start:seen, at : at + HEAD_SIZE]
            scores = dot(key[:seen], query, ((1,), (1,)))
            scores = masked(scores, first_ref[0, :, start:seen], start)
            top = jnp.max(scores, axis=0, keepdims=True)
            weights = jnp.exp2((scores - top) * factor)
            mass = jnp.sum(weights, axis=0, keepdims=True)
            probs = (weights * (1.0 / mass)).astype(bf16)
            out = dot(value_t[:, :seen], probs).T
            stat_ref[0, head : head + 1, start:seen] = top * factor + jnp.log2(mass)
            o_all[pl.ds(slot * length + start, ROW_STEP), at : at + HEAD_SIZE] = out.astype(bf16)

    @pl.when(slot == pl.num_programs(0) - 1)
    def _():
        each = o0.shape[0]
        for k, ref in enumerate((o0, o1, o2, o3)):
            ref[...] = spread_rows(perm_ref, o_all[...], k * each, each).astype(bf16)


def attend(qkv, first, perm_row, each):
    slots, _, length = first.shape
    rows, cols = qkv.shape
    third = cols // 3
    piece = pl.BlockSpec((each, third), lambda i: (0, 0))
    return pl.pallas_call(
        attend_kernel,
        grid=(slots,),
        in_specs=[
            pl.BlockSpec((length, cols), lambda i: (i, 0)),
            pl.BlockSpec((1, 1, length), lambda i: (i, 0, 0)),
            pl.BlockSpec((1, rows), lambda i: (0, 0)),
        ],
        out_specs=[piece] * 4 + [pl.BlockSpec((1, 8, length), lambda i: (i, 0, 0))],
        out_shape=[jax.ShapeDtypeStruct((each, third), bf16)] * 4
        + [jax.ShapeDtypeStruct((slots, 8, length), f32)],
        scratch_shapes=[pltpu.VMEM((rows, third), bf16)],
        name="att",
    )(qkv, first, perm_row)


def attend_back_kernel(
    qkv_ref, first_ref, perm_ref, d0, d1, d2, d3, stat_ref, cos_ref, sin_ref, out_ref, acc, given
):
    length, cols = qkv_ref.shape
    third = cols // 3
    scale = HEAD_SIZE ** (-0.5)
    factor = scale * LOG2E
    for start in range(0, length, ROW_STEP):
        wanted = perm_ref[start : start + ROW_STEP, :]
        given[start : start + ROW_STEP, :] = pick_rows(wanted, (d0, d1, d2, d3)).astype(bf16)
    acc[:, third:] = jnp.zeros((length, 2 * third), f32)
    for head in range(third // HEAD_SIZE):
        at = head * HEAD_SIZE
        key = qkv_ref[:, third + at : third + at + HEAD_SIZE]
        value = qkv_ref[:, 2 * third + at : 2 * third + at + HEAD_SIZE]
        key_t = key.T
        for start in range(0, length, ROW_STEP):
            seen = start + ROW_STEP
            query = qkv_ref[start:seen, at : at + HEAD_SIZE]
            grad = given[start:seen, at : at + HEAD_SIZE]
            scores = dot(key[:seen], query, ((1,), (1,)))
            scores = masked(scores, first_ref[0, :, start:seen], start)
            probs = jnp.exp2(scores * factor - stat_ref[0, head : head + 1, start:seen])
            grad_probs = dot(value[:seen], grad, ((1,), (1,)))
            delta = jnp.sum(probs * grad_probs, axis=0, keepdims=True)
            grad_scores = (probs * (grad_probs - delta)).astype(bf16)
            acc[start:seen, at : at + HEAD_SIZE] = dot(key_t[:, :seen], grad_scores).T
            acc[:seen, third + at : third + at + HEAD_SIZE] += dot(grad_scores, query)
            acc[:seen, 2 * third + at : 2 * third + at + HEAD_SIZE] += dot(
                probs.astype(bf16), grad
            )
    cosine = cos_ref[...]
    sine = -sin_ref[...]
    for start in range(0, 2 * third, LANES):
        out_ref[:, start : start + LANES] = turn(
            acc[:, start : start + LANES] * scale, cosine, sine
        ).astype(bf16)
    out_ref[:, 2 * third :] = acc[:, 2 * third :].astype(bf16)


def attend_back(qkv, first, perm_col, grads, stat, cosine, sine):
    slots, _, length = first.shape
    rows, cols = qkv.shape
    third = cols // 3
    piece = pl.BlockSpec(grads[0].shape, lambda i: (0, 0))
    return pl.pallas_call(
        attend_back_kernel,
        grid=(slots,),
        in_specs=[
            pl.BlockSpec((length, cols), lambda i: (i, 0)),
            pl.BlockSpec((1, 1, length), lambda i: (i, 0, 0)),
            pl.BlockSpec((length, 1), lambda i: (i, 0)),
        ]
        + [piece] * 4
        + [
            pl.BlockSpec((1, 8, length), lambda i: (i, 0, 0)),
            pl.BlockSpec((length, LANES), lambda i: (i, 0)),
            pl.BlockSpec((length, LANES), lambda i: (i, 0)),
        ],
        out_specs=pl.BlockSpec((length, cols), lambda i: (i, 0)),
        out_shape=jax.ShapeDtypeStruct((rows, cols), bf16),
        scratch_shapes=[pltpu.VMEM((length, cols), f32), pltpu.VMEM((length, third), bf16)],
        name="att_b",
    )(qkv, first, perm_col, *grads, stat, cosine, sine)


def out_weights_kernel(grad_ref, *refs):
    grad = grad_ref[...]
    for k in range(4):
        refs[4 + k][...] = dot(grad, refs[k][...], ((0,), (0,))).astype(bf16)


def out_weights(grad, heads):
    width = grad.shape[1]
    cols = heads[0].shape[1]
    return pl.pallas_call(
        out_weights_kernel,
        out_shape=[jax.ShapeDtypeStruct((width, cols), bf16)] * 4,
        name="wout",
    )(grad, *heads)


def unproject(dqkv, perm_row, w, each, first):
    rows, cols = dqkv.shape
    width = w.shape[1]
    third = w.shape[2]

    def kernel(dqkv_ref, perm_ref, w_ref, a_ref, b_ref):
        for k, out_ref in ((first + 1, b_ref), (first, a_ref)):
            start = k * each + pl.program_id(0) * ROW_STEP
            picked = spread_rows(perm_ref, dqkv_ref[...], start, ROW_STEP).astype(bf16)
            total = dot(picked[:, :third], w_ref[0], ((1,), (1,)))
            total += dot(picked[:, third : 2 * third], w_ref[1], ((1,), (1,)))
            total += dot(picked[:, 2 * third :], w_ref[2], ((1,), (1,)))
            out_ref[...] = total.astype(bf16)

    return pl.pallas_call(
        kernel,
        grid=(each // ROW_STEP,),
        in_specs=[
            pl.BlockSpec((rows, cols), lambda i: (0, 0)),
            pl.BlockSpec((1, rows), lambda i: (0, 0)),
            pl.BlockSpec((3,) + w.shape[1:], lambda i: (0, 0, 0)),
        ],
        out_specs=[pl.BlockSpec((ROW_STEP, width), lambda i: (i, 0))] * 2,
        out_shape=[jax.ShapeDtypeStruct((each, width), bf16)] * 2,
    )(dqkv, perm_row, w)


def hop(value, axis, bit):
    count = lax.axis_size(axis)
    return lax.ppermute(value, axis, [(i, i ^ bit) for i in range(count)])


def gather_tensor(value):
    near = hop(value, TENSOR, 1)
    far = hop(value, TENSOR, 2)
    cross = hop(far, TENSOR, 1)
    return [value, near, far, cross]


def exchange_tensor(pieces):
    out = [pieces[0], hop(pieces[1], TENSOR, 1)]
    return out + [hop(pieces[k], TENSOR, k) for k in (2, 3)]


def fold_over(pieces):
    over = hop(pieces[1].astype(bf16), TENSOR, 1)
    return (pieces[0].astype(f32) + over.astype(f32)).astype(bf16)


def fold_far(own, beside, outward):
    back = hop(outward, TENSOR, 2)
    return [own, hop(beside.astype(bf16), TENSOR, 1), back]


def scatter_tensor(pieces):
    return fold_far(pieces[0], pieces[1], fold_over(pieces[2:]))


def add_up(terms):
    total = terms[0].astype(f32)
    for term in terms[1:]:
        total = total + term.astype(f32)
    return total


def total_all(value):
    for axis in (TENSOR, DP):
        bit = 1
        while bit < lax.axis_size(axis):
            value = value + hop(value, axis, bit)
            bit *= 2
    return value


def gather_dp(value):
    return lax.all_gather(value, DP, axis=0, tiled=True)


def scatter_dp(value):
    return lax.psum_scatter(value.astype(bf16), DP, scatter_dimension=0, tiled=True).astype(f32)


def gather_dp_steps(value, waiting):
    count = lax.axis_size(DP)
    kinds, share, cols = value.shape
    if count > 8:
        return lax.all_gather(value, DP, axis=1, tiled=True), waiting
    place = lax.axis_index(DP)
    bit = count // 2
    axis = 1
    while bit:
        other = hop(value, DP, bit)
        upper = jnp.where((place & bit) > 0, 1, 0)
        shape = value.shape[:axis] + (2,) + value.shape[axis:]
        mine = lax.broadcasted_iota(jnp.int32, shape, axis) == upper
        value = jnp.where(mine, jnp.expand_dims(value, axis), jnp.expand_dims(other, axis))
        if bit == 2:
            waiting, value = lax.optimization_barrier((waiting, value))
        axis += 1
        bit //= 2
    return value.reshape(kinds, count * share, cols), waiting


def scatter_dp_parts(parts):
    count = lax.axis_size(DP)
    parts = parts[:1] + [hop(parts[k], DP, k) for k in range(1, count)]
    total = parts[0].astype(f32)
    for part in parts[1:]:
        total = total + part.astype(f32)
    return total


def qkv_weights_kernel(place_ref, normed_ref, dqkv_ref, w_ref, other_ref, *refs):
    parts, gain_ref, acc = refs[:-2], refs[-2], refs[-1]
    step = pl.program_id(0)
    cols = acc.shape[1]
    part = dot(normed_ref[...], dqkv_ref[...], ((0,), (0,)))

    @pl.when(step == 0)
    def _():
        acc[...] = part

    @pl.when(step > 0)
    def _():
        acc[...] += part

    @pl.when(step == pl.num_programs(0) - 1)
    def _():
        gain = None
        third = w_ref.shape[2]
        for c in range(3):
            term = acc[:, c * third : (c + 1) * third] * w_ref[c].astype(f32)
            gain = term if gain is None else gain + term
        gain_ref[...] = jnp.sum(gain, axis=1, keepdims=True)
        share = acc.shape[0] // len(parts)
        for k, ref in enumerate(parts):
            at = pl.multiple_of((place_ref[0] ^ k) * share, 8)
            ref[:, :cols] = acc[pl.ds(at, share), :].astype(bf16)
            ref[:, cols:] = other_ref[pl.ds(at, share), :].astype(bf16)


def qkv_weights(normed, dqkv, w, other, place, count):
    rows, width = normed.shape
    cols = dqkv.shape[1]
    extra = other.shape[1]
    step = 2 * ROW_STEP
    share = width // count
    return pl.pallas_call(
        qkv_weights_kernel,
        grid=(rows // step,),
        in_specs=[
            pl.BlockSpec(memory_space=pltpu.SMEM),
            pl.BlockSpec((step, width), lambda i: (i, 0)),
            pl.BlockSpec((step, cols), lambda i: (i, 0)),
            pl.BlockSpec((3,) + w.shape[1:], lambda i: (0, 0, 0)),
            pl.BlockSpec(other.shape, lambda i: (0, 0)),
        ],
        out_specs=[pl.BlockSpec((share, cols + extra), lambda i: (0, 0))] * count
        + [pl.BlockSpec((width, 1), lambda i: (0, 0))],
        out_shape=[jax.ShapeDtypeStruct((share, cols + extra), bf16)] * count
        + [jax.ShapeDtypeStruct((width, 1), f32)],
        scratch_shapes=[pltpu.VMEM((width, cols), f32)],
        name="wqkv",
    )(place, normed, dqkv, w, other)


def layer(
    hidden_in,
    earlier,
    gain_attn,
    gain_mlp,
    w_qkv,
    w_out,
    w_up,
    w_down,
    mix_weights,
    lengths,
    slot_perm,
    grad_out,
):
    tensor_place = lax.axis_index(TENSOR)
    own_rows, width = hidden_in.shape
    slot_count = lengths.shape[0]
    group_rows = slot_perm.shape[0]
    slot_len = group_rows // slot_count
    shard_d = w_qkv.shape[0]
    head_cols = w_qkv.shape[2]

    hidden = hidden_in.astype(f32)
    normed_attn = layer_norm(hidden, gain_attn).astype(bf16)
    attn_pieces = gather_tensor(normed_attn)
    planes = jnp.concatenate([jnp.transpose(w_qkv, (1, 0, 2)), w_out.T[None]], axis=0)
    mlp_shard = jnp.concatenate([w_up, w_down.T], axis=1)
    full_qkv, mlp_shard = gather_dp_steps(planes, mlp_shard)
    updown = gather_dp(mlp_shard)
    out_pieces = gather_tensor(full_qkv[3])

    first, position = slot_layout(lengths, slot_len)
    first = first.reshape(slot_count, 1, slot_len)
    cosine, sine = angle_tables(position.reshape(-1))
    perm = ((slot_perm // own_rows) ^ tensor_place) * own_rows + slot_perm % own_rows
    perm_col = perm[:, None]
    perm_row = perm[None, :]

    cotangent = grad_out.astype(f32)
    own_grad = mix_weights[4] * cotangent
    grad_pieces = gather_tensor(own_grad.astype(bf16))

    normed_slot = to_slots(attn_pieces, perm_col)
    qkv = project(normed_slot, full_qkv, cosine, sine)
    *attended, stat = attend(qkv, first, perm_row, own_rows)
    attended = exchange_tensor(attended)
    early_in, early_grad, attended[1] = lax.optimization_barrier((earlier, grad_out, attended[1]))
    grad_earlier, prior, prior_terms = mix_early(mix_weights, early_in, early_grad)
    after_attn, normed_mlp = project_out(hidden_in, gain_mlp, attended, out_pieces)
    mlp_rows = gather_tensor(normed_mlp)

    dn0, hid0, du0, dn1, hid1, du1 = mlp(mlp_rows[:2], grad_pieces[:2], updown)
    dn2, hid2, du2, dn3, hid3, du3 = mlp(mlp_rows[2:], grad_pieces[2:], updown)
    mlp_terms = scatter_tensor([dn0, dn1, dn2, dn3])
    hids = [hid0, hid1, hid2, hid3]
    mlp_total = scatter_tensor(mlp_out(hids, updown))
    mlp_grads, down_terms = mlp_weights(
        mlp_rows, grad_pieces, hids, [du0, du1, du2, du3], updown
    )
    grad_updown = scatter_dp(mlp_grads)
    units = w_up.shape[1]
    grad_up = grad_updown[:, :units]
    grad_down_t = grad_updown[:, units:]

    grad_after, grad_low, gain_rows, own_terms, *grad_heads = mid_back(
        mix_weights, after_attn, gain_mlp, mlp_terms, grad_out, out_pieces
    )
    grad_gain_mlp = jnp.sum(gain_rows, axis=(0, 1))
    grad_attended = exchange_tensor(grad_heads)
    out_scattered = add_up(scatter_tensor(out_weights(grad_low, attended)))

    dqkv = attend_back(qkv, first, perm_col, grad_attended, stat, cosine, sine)
    part2, part3 = unproject(dqkv, perm_row, full_qkv, own_rows, 2)
    outward = fold_over([part2, part3])
    dp_count = lax.axis_size(DP)
    small = dp_count <= 8
    *parts, gain_partial = qkv_weights(
        normed_slot,
        dqkv,
        full_qkv,
        out_scattered,
        jnp.full((1,), lax.axis_index(DP) if small else 0, jnp.int32),
        dp_count if small else 1,
    )
    part0, part1 = unproject(dqkv, perm_row, full_qkv, own_rows, 0)
    attn_terms = fold_far(part0, part1, outward)
    late_prior, part1 = lax.optimization_barrier((prior, part1))
    if small:
        grad_both = scatter_dp_parts(parts)
    else:
        grad_both = scatter_dp(parts[0])
    grad_qkv = grad_both[:, : 3 * head_cols]
    grad_out_t = grad_both[:, 3 * head_cols :]
    grad_gain_attn = gain_partial[:, 0] / gain_attn

    grad_hidden = last_back(hidden_in, gain_attn, attn_terms, grad_after)

    mixed = mix_late(mix_weights, after_attn, mlp_total, late_prior)
    last_term = jnp.sum(own_terms) + jnp.sum(down_terms) / mix_weights[4]
    mix_terms = jnp.concatenate([jnp.sum(prior_terms, axis=(0, 2)), last_term[None]])
    spare = -(2 * width + 5) % 1024
    packed = jnp.concatenate(
        [grad_gain_attn, grad_gain_mlp, mix_terms, jnp.zeros((spare,), f32)]
    )
    packed = total_all(packed.reshape(-1, LANES)).reshape(-1)
    return (
        mixed,
        grad_hidden,
        grad_earlier,
        packed[:width],
        packed[width : 2 * width],
        grad_qkv.reshape(shard_d, 3, head_cols),
        grad_out_t.T,
        grad_up,
        grad_down_t.T,
        packed[2 * width : 2 * width + 5],
    )


def solution(mesh):
    rows = P((DP, TENSOR), None)
    layers = P(None, (DP, TENSOR), None)
    return jax.shard_map(
        layer,
        mesh=mesh,
        in_specs=(
            rows,
            layers,
            P(),
            P(),
            P(DP, None, TENSOR),
            P(TENSOR, DP),
            P(DP, TENSOR),
            P(TENSOR, DP),
            P(),
            P(DP, None),
            P(DP),
            rows,
        ),
        out_specs=(
            rows,
            rows,
            layers,
            P(),
            P(),
            P(DP, None, TENSOR),
            P(TENSOR, DP),
            P(DP, TENSOR),
            P(TENSOR, DP),
            P(),
        ),
        check_vma=False,
    )
```

profile of v0, /device:TPU:23, one launch (start us, length us, event | category | flops | bytes accessed | tf_op | source)
XLA Modules:
  0.0 361.7 jit_solution(10355907394528983363)
XLA Ops:
  11.0 6.1 %collective-permute-done.3 = bf16[4,96,192]{2,1,0:T(8,128)(2,1)S(1)} collective-permute-done((bf16[4,96,192]{2,1,0:T(8,128)(2,1)S(1)}, bf16[4,96,192]{2,1,0:T(8,128)(2,1)S(1)}, u32[]{:S(2)}, u32[]{:S(2)}) %collective-permute-start.3) | collective-permute-done | bytes 147488 | tf_op jit(solution)/shard_map/ppermute | solution.py:558
  17.2 5.3 %collective-permute-start.4 = (bf16[4,2,96,192]{3,2,1,0:T(8,128)(2,1)S(1)}, bf16[4,2,96,192]{3,2,1,0:T(8,128)(2,1)S(1)}, u32[]{:S(2)}, u32[]{:S(2)}) collective-permute-start(bf16[4,2,96,192]{3,2,1,0:T(8,128)(2,1)S(1)} %broadcast_select_fusion.2), channel_id=1, source_target_pairs={{0,8},{4,12},{8,0},{12,4},{16,24},{20,28},{24,16},{28,20},{1,9},{5... | collective-permute-start | bytes 884744 | tf_op jit(solution)/shard_map/ppermute | solution.py:558
  23.3 8.3 %collective-permute-done.4 = bf16[4,2,96,192]{3,2,1,0:T(8,128)(2,1)S(1)} collective-permute-done((bf16[4,2,96,192]{3,2,1,0:T(8,128)(2,1)S(1)}, bf16[4,2,96,192]{3,2,1,0:T(8,128)(2,1)S(1)}, u32[]{:S(2)}, u32[]{:S(2)}) %collective-permute-start.4) | collective-permute-done | bytes 294944 | tf_op jit(solution)/shard_map/ppermute | solution.py:558
  35.4 15.9 %collective-permute-done.1.n2 = bf16[512,768]{1,0:T(8,128)(2,1)} collective-permute-done((bf16[512,768]{1,0:T(8,128)(2,1)}, bf16[512,768]{1,0:T(8,128)(2,1)}, u32[]{:S(2)}, u32[]{:S(2)}) %collective-permute-start.1) | collective-permute-done | bytes 786464 | tf_op jit(solution)/shard_map/ppermute | solution.py:558
  56.4 3.7 %fusion.5 = (f32[2048,32]{1,0:T(8,128)S(1)}, f32[2048,32]{1,0:T(8,128)S(1)}, f32[2048,32]{1,0:T(8,128)S(1)}) fusion(f32[32]{0:T(128)S(1)} %negate_power_fusion, f32[2048]{0:T(1024)S(1)} %bitcast.47), kind=kLoop, calls=%fused_computation.21 | loop fusion | flops 131072 | bytes 794752 | tf_op jit(solution)/shard_map/neg | solution.py:45
  60.2 3.0 pad_maximum_fusion
  73.6 11.3 %order.1.normed_ref = bf16[2048,768]{1,0:T(8,128)(2,1)} custom-call(bf16[512,768]{1,0:T(8,128)(2,1)} %fusion.4.n0, bf16[512,768]{1,0:T(8,128)(2,1)} %collective-permute-done.n1, bf16[512,768]{1,0:T(8,128)(2,1)} %collective-permute-done.1.n2, bf16[512,768]{1,0:T(8,128)(2,1)} %collective-permute-done.2.n3, s32[2048,1]{1,0:T(8,128)} %copy.37.perm_ref), custom_call_target="tpu_custom_call" | custom-call | tf_op jit(solution)/shard_map/order/pallas_call | solution.py:82
  84.9 7.6 %proj.1.qkv_ref = bf16[2048,576]{1,0:T(8,128)(2,1)} custom-call(bf16[2048,768]{1,0:T(8,128)(2,1)} %order.1.normed_ref, bf16[4,768,192]{2,1,0:T(8,128)(2,1)} %bitcast_select_fusion.w_ref, f32[2048,128]{1,0:T(8,128)} %get-tuple-element.173.cos_ref, f32[2048,128]{1,0:T(8,128)} %get-tuple-element.174.sin_ref), custom_call_target="tpu_custom_call" | custom-call | tf_op jit(solution)/shard_map/proj/pallas_call | solution.py:109
  92.5 17.7 %att.1 = (bf16[512,192]{1,0:T(8,128)(2,1)}, bf16[512,192]{1,0:T(8,128)(2,1)}, bf16[512,192]{1,0:T(8,128)(2,1)}, bf16[512,192]{1,0:T(8,128)(2,1)}, f32[2,8,1024]{2,1,0:T(8,128)}) custom-call(bf16[2048,576]{1,0:T(8,128)(2,1)} %proj.1.qkv_ref, s32[2,1,1024]{2,1,0:T(1,128)} %reshape.83.first_ref, s32[1,2048]{1,0:T(1,128)} %bitcast.40), custom_call_target="tpu_custom_call" | custom-call | tf_op jit(solution)/shard_map/att/pallas_call | solution.py:431
  114.4 3.6 collective-permute-done.7.refs_2_
  117.9 7.1 %collective-permute-done.8.refs_3_ = bf16[512,192]{1,0:T(8,128)(2,1)S(1)} collective-permute-done((bf16[512,192]{1,0:T(8,128)(2,1)}, bf16[512,192]{1,0:T(8,128)(2,1)S(1)}, u32[]{:S(2)}, u32[]{:S(2)}) %collective-permute-start.8) | collective-permute-done | bytes 196640 | tf_op jit(solution)/shard_map/ppermute | solution.py:558
  125.7 4.2 %proj_o.1 = (f32[512,768]{1,0:T(8,128)}, bf16[512,768]{1,0:T(8,128)(2,1)}) custom-call(bf16[512,768]{1,0:T(8,128)(2,1)} %value_ref.3, f32[1,768]{1,0:T(1,128)} %broadcast_in_dim.102.gain_ref, bf16[512,192]{1,0:T(8,128)(2,1)} %get-tuple-element.70.refs_0_, bf16[512,192]{1,0:T(8,128)(2,1)} %copy-done.13, bf16[512,192]{1,0:T(8,128)(2,1)} %copy-done.14, ...), custom_call_target="tpu_custom_call" | custom-call | tf_op jit(solution)/shard_map/proj_o/pallas_call | solution.py:218
  131.6 8.8 %collective-permute-done.16.ga_ref.refs_6_ = bf16[512,768]{1,0:T(8,128)(2,1)S(1)} collective-permute-done((bf16[512,768]{1,0:T(8,128)(2,1)S(1)}, bf16[512,768]{1,0:T(8,128)(2,1)S(1)}, u32[]{:S(2)}, u32[]{:S(2)}) %collective-permute-start.16) | collective-permute-done | bytes 786464 | tf_op jit(solution)/shard_map/ppermute | solution.py:558
  142.6 14.7 %collective-permute-done.14.a_ref.refs_2_ = bf16[512,768]{1,0:T(8,128)(2,1)S(1)} collective-permute-done((bf16[512,768]{1,0:T(8,128)(2,1)}, bf16[512,768]{1,0:T(8,128)(2,1)S(1)}, u32[]{:S(2)}, u32[]{:S(2)}) %collective-permute-start.14) | collective-permute-done | bytes 786464 | tf_op jit(solution)/shard_map/ppermute | solution.py:558
  159.4 8.1 %shard_map.195 = (bf16[512,768]{1,0:T(8,128)(2,1)}, bf16[512,768]{1,0:T(8,128)(2,1)}, bf16[512,768]{1,0:T(8,128)(2,1)}, bf16[512,768]{1,0:T(8,128)(2,1)}, bf16[5...) custom-call(bf16[512,768]{1,0:T(8,128)(2,1)} %get-tuple-element.76.a_ref.refs_0_, ...), custom_call_target="tpu_custom_call" | custom-call | tf_op jit(solution)/shard_map/pallas_call | solution.py:304
  167.5 7.9 %shard_map.196 = (bf16[512,768]{1,0:T(8,128)(2,1)}, bf16[512,768]{1,0:T(8,128)(2,1)}, bf16[512,768]{1,0:T(8,128)(2,1)}, bf16[512,768]{1,0:T(8,128)(2,1)}, bf16[5...) custom-call(bf16[512,768]{1,0:T(8,128)(2,1)} %copy-done.7, bf16[512,768]{1,0:T(8,128)(2,1)} %collective-permute-done.15.b_ref.refs_3_, ...), custom_call_target="tpu_custom_call" | custom-call | tf_op jit(solution)/shard_map/pallas_call | solution.py:304
  175.4 10.9 %wmlp.1 = (bf16[768,1536]{1,0:T(8,128)(2,1)}, f32[1,768]{1,0:T(1,128)}) custom-call(bf16[512,768]{1,0:T(8,128)(2,1)} %get-tuple-element.76.a_ref.refs_0_, bf16[512,768]{1,0:T(8,128)(2,1)} %collective-permute-done.12.b_ref.refs_1_, bf16[512,768]{1,0:T(8,128)(2,1)} %copy-done.7, bf16[512,768]{1,0:T(8,128)(2,1)} %collective-permute-done.15.b_ref.refs_3_, ...), custom_call_target="tpu_custom_call" | custom-call | tf_op jit(solution)/shard_map/wmlp/pallas_call | solution.py:366
  191.1 5.6 %mlp_out.1 = (bf16[512,768]{1,0:T(8,128)(2,1)}, bf16[512,768]{1,0:T(8,128)(2,1)}, bf16[512,768]{1,0:T(8,128)(2,1)}, bf16[512,768]{1,0:T(8,128)(2,1)}) custom-call(bf16[512,768]{1,0:T(8,128)(2,1)} %get-tuple-element.78.h0.refs_8_, bf16[512,768]{1,0:T(8,128)(2,1)} %get-tuple-element.79.h1.refs_9_, bf16[512,768]{1,0:T(8,128)(2,1)} %get-tuple-element.80.h2.refs_10_, ...), custom_call_target="tpu_custom_call" | custom-call | tf_op jit(solution)/shard_map/mlp_out/pallas_call | solution.py:325
  197.2 11.9 %collective-permute-done.23.c_ref = bf16[512,768]{1,0:T(8,128)(2,1)S(1)} collective-permute-done((bf16[512,768]{1,0:T(8,128)(2,1)S(1)}, bf16[512,768]{1,0:T(8,128)(2,1)S(1)}, u32[]{:S(2)}, u32[]{:S(2)}) %collective-permute-start.23) | collective-permute-done | bytes 786464 | tf_op jit(solution)/shard_map/ppermute | solution.py:558
  210.0 6.3 %mid_b.1 = (f32[512,768]{1,0:T(8,128)}, bf16[512,768]{1,0:T(8,128)(2,1)}, f32[2,1,768]{2,1,0:T(1,128)}, f32[2,1,768]{2,1,0:T(1,128)}, bf16[512,192]{1,0:T(8,128)...) custom-call(f32[5]{0:T(128)} %mix_ref.5, ...), custom_call_target="tpu_custom_call" | custom-call | tf_op jit(solution)/shard_map/mid_b/pallas_call | solution.py:161
  216.3 3.4 wout.1
  229.4 6.1 %collective-permute-done.26.d3 = bf16[512,192]{1,0:T(8,128)(2,1)S(1)} collective-permute-done((bf16[512,192]{1,0:T(8,128)(2,1)}, bf16[512,192]{1,0:T(8,128)(2,1)S(1)}, u32[]{:S(2)}, u32[]{:S(2)}) %collective-permute-start.26) | collective-permute-done | bytes 196640 | tf_op jit(solution)/shard_map/ppermute | solution.py:558
  236.1 22.1 %att_b.1.dqkv_ref = bf16[2048,576]{1,0:T(8,128)(2,1)} custom-call(bf16[2048,576]{1,0:T(8,128)(2,1)} %proj.1.qkv_ref, s32[2,1,1024]{2,1,0:T(1,128)} %reshape.83.first_ref, s32[2048,1]{1,0:T(8,128)} %copy.37.perm_ref, bf16[512,192]{1,0:T(8,128)(2,1)} %get-tuple-element.93.d0, bf16[512,192]{1,0:T(8,128)(2,1)} %copy-done.25, bf16[512,192]{1,0:T(8,128)(2,1)} %copy-done.26, ...), custom_call_target="tpu_custom_call" | custom-call | tf_op jit(solution)/shard_map/att_b/pallas_call | solution.py:492
  258.3 8.2 %shard_map.198 = (bf16[512,768]{1,0:T(8,128)(2,1)}, bf16[512,768]{1,0:T(8,128)(2,1)}) custom-call(bf16[2048,576]{1,0:T(8,128)(2,1)} %att_b.1.dqkv_ref, s32[1,2048]{1,0:T(1,128)} %bitcast.41, bf16[4,768,192]{2,1,0:T(8,128)(2,1)} %bitcast_select_fusion.w_ref), custom_call_target="tpu_custom_call" | custom-call | tf_op jit(solution)/shard_map/pallas_call | solution.py:543
  266.5 4.3 %mix_e.1 = (bf16[4,512,768]{2,1,0:T(8,128)(2,1)}, f32[512,768]{1,0:T(8,128)}, f32[2,4,768]{2,1,0:T(4,128)}) custom-call(f32[5]{0:T(128)} %mix_ref.5, bf16[4,512,768]{2,1,0:T(8,128)(2,1)} %earlier_ref, bf16[512,768]{1,0:T(8,128)(2,1)} %grad_ref.2), custom_call_target="tpu_custom_call" | custom-call | tf_op jit(solution)/shard_map/mix_e/pallas_call | solution.py:250
  277.2 8.2 %wqkv.1 = (bf16[96,768]{1,0:T(8,128)(2,1)}, bf16[96,768]{1,0:T(8,128)(2,1)}, bf16[96,768]{1,0:T(8,128)(2,1)}, bf16[96,768]{1,0:T(8,128)(2,1)}, bf16[96,768]{1,0:...) custom-call(s32[1]{0:T(128)} %bitcast.10.place_ref, ...), custom_call_target="tpu_custom_call" | custom-call | tf_op jit(solution)/shard_map/wqkv/pallas_call | solution.py:676
  293.8 8.0 %shard_map.197 = (bf16[512,768]{1,0:T(8,128)(2,1)}, bf16[512,768]{1,0:T(8,128)(2,1)}) custom-call(bf16[2048,576]{1,0:T(8,128)(2,1)} %att_b.1.dqkv_ref, s32[1,2048]{1,0:T(1,128)} %bitcast.42, bf16[4,768,192]{2,1,0:T(8,128)(2,1)} %bitcast_select_fusion.w_ref), custom_call_target="tpu_custom_call" | custom-call | tf_op jit(solution)/shard_map/pallas_call | solution.py:543
  310.6 4.1 %collective-permute-start.27 = (bf16[512,768]{1,0:T(8,128)(2,1)}, bf16[512,768]{1,0:T(8,128)(2,1)S(1)}, u32[]{:S(2)}, u32[]{:S(2)}) collective-permute-start(bf16[512,768]{1,0:T(8,128)(2,1)} %get-tuple-element.98), channel_id=1, source_target_pairs={{0,1},{1,0},{2,3},{3,2},{4,5},{5,4},{6,7},{7,6},{8,9},{9,8},{10,11... | collective-permute-start | bytes 2359304 | tf_op jit(solution)/shard_map/ppermute | solution.py:558
  316.6 3.6 mix_l.1
  327.8 12.3 %collective-permute-done.43 = bf16[96,768]{1,0:T(8,128)(2,1)S(1)} collective-permute-done((bf16[96,768]{1,0:T(8,128)(2,1)}, bf16[96,768]{1,0:T(8,128)(2,1)S(1)}, u32[]{:S(2)}, u32[]{:S(2)}) %collective-permute-start.43) | collective-permute-done | bytes 147488 | tf_op jit(solution)/shard_map/ppermute | solution.py:558
  340.2 4.1 %collective-permute-done.44 = bf16[96,768]{1,0:T(8,128)(2,1)S(1)} collective-permute-done((bf16[96,768]{1,0:T(8,128)(2,1)}, bf16[96,768]{1,0:T(8,128)(2,1)S(1)}, u32[]{:S(2)}, u32[]{:S(2)}) %collective-permute-start.44) | collective-permute-done | bytes 147488 | tf_op jit(solution)/shard_map/ppermute | solution.py:558
  348.3 3.8 %last_b.1 = bf16[512,768]{1,0:T(8,128)(2,1)} custom-call(bf16[512,768]{1,0:T(8,128)(2,1)} %value_ref.3, f32[1,768]{1,0:T(1,128)} %broadcast_in_dim.115.gain_ref, bf16[512,768]{1,0:T(8,128)(2,1)} %get-tuple-element.100.a_ref, bf16[512,768]{1,0:T(8,128)(2,1)} %copy-done.23, bf16[512,768]{1,0:T(8,128)(2,1)} %collective-permute-done.29.c_ref, ...), custom_call_target="tpu_custom_call" | custom-call | tf_op jit(solution)/shard_map/last_b/pallas_call | solution.py:195
  (229 shorter events, 88.7 us)
Async XLA Ops:
  7.2 151.4 %all-gather.2.cloned.1.call-start = ((), (), s32[]{:S(2)}) async-start(), calls=%async_computation.1 | async-start | bytes 2654208 | tf_op jit(solution)/shard_map/all_gather | solution.py:604
  17.2 14.3 %collective-permute-start.4 = (bf16[4,2,96,192]{3,2,1,0:T(8,128)(2,1)S(1)}, bf16[4,2,96,192]{3,2,1,0:T(8,128)(2,1)S(1)}, u32[]{:S(2)}, u32[]{:S(2)}) collective-permute-start(bf16[4,2,96,192]{3,2,1,0:T(8,128)(2,1)S(1)} %broadcast_select_fusion.2), channel_id=1, source_target_pairs={{0,8},{4,12},{8,0},{12,4},{16,24},{20,28},{24,16},{28,20},{1,9},{5... | collective-permute-start | bytes 884744 | tf_op jit(solution)/shard_map/ppermute | solution.py:558
  31.7 320.4 %reduce-scatter.2.cloned.1.call-start = ((), (), s32[]{:S(2)}) async-start(), calls=%async_computation.2 | async-start | bytes 2654208 | tf_op jit(solution)/shard_map/reduce_scatter | solution.py:608
  32.9 18.3 %collective-permute-start.1 = (bf16[512,768]{1,0:T(8,128)(2,1)}, bf16[512,768]{1,0:T(8,128)(2,1)}, u32[]{:S(2)}, u32[]{:S(2)}) collective-permute-start(bf16[512,768]{1,0:T(8,128)(2,1)} %fusion.4.n0), channel_id=1, source_target_pairs={{0,2},{1,3},{2,0},{3,1},{4,6},{5,7},{6,4},{7,5},{8,10},{9,11},{10,... | collective-permute-start | bytes 2359304 | tf_op jit(solution)/shard_map/ppermute | solution.py:558
  33.2 21.0 %collective-permute-start.5 = (bf16[4,2,2,96,192]{4,3,2,1,0:T(8,128)(2,1)S(1)}, bf16[4,2,2,96,192]{4,3,2,1,0:T(8,128)(2,1)S(1)}, u32[]{:S(2)}, u32[]{:S(2)}) collective-permute-start(bf16[4,2,2,96,192]{4,3,2,1,0:T(8,128)(2,1)S(1)} %broadcast_select_fusion), channel_id=1, source_target_pairs={{0,4},{4,0},{8,12},{12,8},{16,20},{20,16},{24,28},{28,24},{1,5},{5... | collective-permute-start | bytes 1769480 | tf_op jit(solution)/shard_map/ppermute | solution.py:558
  33.4 40.1 %collective-permute-start = (bf16[512,768]{1,0:T(8,128)(2,1)}, bf16[512,768]{1,0:T(8,128)(2,1)}, u32[]{:S(2)}, u32[]{:S(2)}) collective-permute-start(bf16[512,768]{1,0:T(8,128)(2,1)} %fusion.4.n0), channel_id=1, source_target_pairs={{0,1},{1,0},{2,3},{3,2},{4,5},{5,4},{6,7},{7,6},{8,9},{9,8},{10,11... | collective-permute-start | bytes 2359304 | tf_op jit(solution)/shard_map/ppermute | solution.py:558
  51.3 22.3 %collective-permute-start.2 = (bf16[512,768]{1,0:T(8,128)(2,1)}, bf16[512,768]{1,0:T(8,128)(2,1)}, u32[]{:S(2)}, u32[]{:S(2)}) collective-permute-start(bf16[512,768]{1,0:T(8,128)(2,1)} %collective-permute-done.1.n2), channel_id=1, source_target_pairs={{0,1},{1,0},{2,3},{3,2},{4,5},{5,4},{6,7},{7,6},{8,9},{9,8},{10,11... | collective-permute-start | bytes 2359304 | tf_op jit(solution)/shard_map/ppermute | solution.py:558
  55.2 10.5 %collective-permute-start.10 = (bf16[768,192]{1,0:T(8,128)(2,1)S(1)}, bf16[768,192]{1,0:T(8,128)(2,1)}, u32[]{:S(2)}, u32[]{:S(2)}) collective-permute-start(bf16[768,192]{1,0:T(8,128)(2,1)S(1)} %bitcast.34), channel_id=1, source_target_pairs={{0,2},{1,3},{2,0},{3,1},{4,6},{5,7},{6,4},{7,5},{8,10},{9,11},{10,... | collective-permute-start | bytes 884744 | tf_op jit(solution)/shard_map/ppermute | solution.py:558
  63.2 51.1 %collective-permute-start.9 = (bf16[768,192]{1,0:T(8,128)(2,1)S(1)}, bf16[768,192]{1,0:T(8,128)(2,1)S(1)}, u32[]{:S(2)}, u32[]{:S(2)}) collective-permute-start(bf16[768,192]{1,0:T(8,128)(2,1)S(1)} %bitcast.35), channel_id=1, source_target_pairs={{0,1},{1,0},{2,3},{3,2},{4,5},{5,4},{6,7},{7,6},{8,9},{9,8},{10,11... | collective-permute-start | bytes 884744 | tf_op jit(solution)/shard_map/ppermute | solution.py:558
  65.7 48.6 %collective-permute-start.11 = (bf16[768,192]{1,0:T(8,128)(2,1)}, bf16[768,192]{1,0:T(8,128)(2,1)S(1)}, u32[]{:S(2)}, u32[]{:S(2)}) collective-permute-start(bf16[768,192]{1,0:T(8,128)(2,1)} %collective-permute-done.10.refs_6_.refs_2_), channel_id=1, source_target_pairs={{0,1},{1,0},{2,3},{3,2},{4,5},{5,4},{6,7},{7,6},{8,9},{9,8},{10,11... | collective-permute-start | bytes 884744 | tf_op jit(solution)/shard_map/ppermute | solution.py:558
  111.3 13.7 %collective-permute-start.8 = (bf16[512,192]{1,0:T(8,128)(2,1)}, bf16[512,192]{1,0:T(8,128)(2,1)S(1)}, u32[]{:S(2)}, u32[]{:S(2)}) collective-permute-start(bf16[512,192]{1,0:T(8,128)(2,1)} %get-tuple-element.74), channel_id=1, source_target_pairs={{0,3},{1,2},{2,1},{3,0},{4,7},{5,6},{6,5},{7,4},{8,11},{9,10},{10,... | collective-permute-start | bytes 589832 | tf_op jit(solution)/shard_map/ppermute | solution.py:558
  113.2 27.2 %collective-permute-start.16 = (bf16[512,768]{1,0:T(8,128)(2,1)S(1)}, bf16[512,768]{1,0:T(8,128)(2,1)S(1)}, u32[]{:S(2)}, u32[]{:S(2)}) collective-permute-start(bf16[512,768]{1,0:T(8,128)(2,1)S(1)} %multiply_convert_fusion.ga_ref.refs_4_), channel_id=1, source_target_pairs={{0,2},{1,3},{2,0},{3,1},{4,6},{5,7},{6,4},{7,5},{8,10},{9,11},{10,... | collective-permute-start | bytes 2359304 | tf_op jit(solution)/shard_map/ppermute | solution.py:558
  130.0 27.3 %collective-permute-start.14 = (bf16[512,768]{1,0:T(8,128)(2,1)}, bf16[512,768]{1,0:T(8,128)(2,1)S(1)}, u32[]{:S(2)}, u32[]{:S(2)}) collective-permute-start(bf16[512,768]{1,0:T(8,128)(2,1)} %get-tuple-element.76.a_ref.refs_0_), channel_id=1, source_target_pairs={{0,2},{1,3},{2,0},{3,1},{4,6},{5,7},{6,4},{7,5},{8,10},{9,11},{10,... | collective-permute-start | bytes 2359304 | tf_op jit(solution)/shard_map/ppermute | solution.py:558
  131.0 27.5 %collective-permute-start.13 = (bf16[512,768]{1,0:T(8,128)(2,1)S(1)}, bf16[512,768]{1,0:T(8,128)(2,1)S(1)}, u32[]{:S(2)}, u32[]{:S(2)}) collective-permute-start(bf16[512,768]{1,0:T(8,128)(2,1)S(1)} %multiply_convert_fusion.ga_ref.refs_4_), channel_id=1, source_target_pairs={{0,1},{1,0},{2,3},{3,2},{4,5},{5,4},{6,7},{7,6},{8,9},{9,8},{10,11... | collective-permute-start | bytes 2359304 | tf_op jit(solution)/shard_map/ppermute | solution.py:558
  131.1 27.5 %collective-permute-start.12 = (bf16[512,768]{1,0:T(8,128)(2,1)}, bf16[512,768]{1,0:T(8,128)(2,1)}, u32[]{:S(2)}, u32[]{:S(2)}) collective-permute-start(bf16[512,768]{1,0:T(8,128)(2,1)} %get-tuple-element.76.a_ref.refs_0_), channel_id=1, source_target_pairs={{0,1},{1,0},{2,3},{3,2},{4,5},{5,4},{6,7},{7,6},{8,9},{9,8},{10,11... | collective-permute-start | bytes 2359304 | tf_op jit(solution)/shard_map/ppermute | solution.py:558
  140.4 27.1 %collective-permute-start.17 = (bf16[512,768]{1,0:T(8,128)(2,1)S(1)}, bf16[512,768]{1,0:T(8,128)(2,1)}, u32[]{:S(2)}, u32[]{:S(2)}) collective-permute-start(bf16[512,768]{1,0:T(8,128)(2,1)S(1)} %collective-permute-done.16.ga_ref.refs_6_), channel_id=1, source_target_pairs={{0,1},{1,0},{2,3},{3,2},{4,5},{5,4},{6,7},{7,6},{8,9},{9,8},{10,11... | collective-permute-start | bytes 2359304 | tf_op jit(solution)/shard_map/ppermute | solution.py:558
  190.0 19.1 %collective-permute-start.23 = (bf16[512,768]{1,0:T(8,128)(2,1)S(1)}, bf16[512,768]{1,0:T(8,128)(2,1)S(1)}, u32[]{:S(2)}, u32[]{:S(2)}) collective-permute-start(bf16[512,768]{1,0:T(8,128)(2,1)S(1)} %add_convert_fusion.1), channel_id=1, source_target_pairs={{0,2},{1,3},{2,0},{3,1},{4,6},{5,7},{6,4},{7,5},{8,10},{9,11},{10,... | collective-permute-start | bytes 2359304 | tf_op jit(solution)/shard_map/ppermute | solution.py:558
  196.7 27.2 %collective-permute-start.19 = (bf16[512,768]{1,0:T(8,128)(2,1)}, bf16[512,768]{1,0:T(8,128)(2,1)S(1)}, u32[]{:S(2)}, u32[]{:S(2)}) collective-permute-start(bf16[512,768]{1,0:T(8,128)(2,1)} %get-tuple-element.85), channel_id=1, source_target_pairs={{0,1},{1,0},{2,3},{3,2},{4,5},{5,4},{6,7},{7,6},{8,9},{9,8},{10,11... | collective-permute-start | bytes 2359304 | tf_op jit(solution)/shard_map/ppermute | solution.py:558
  221.7 13.7 %collective-permute-start.26 = (bf16[512,192]{1,0:T(8,128)(2,1)}, bf16[512,192]{1,0:T(8,128)(2,1)S(1)}, u32[]{:S(2)}, u32[]{:S(2)}) collective-permute-start(bf16[512,192]{1,0:T(8,128)(2,1)} %get-tuple-element.96), channel_id=1, source_target_pairs={{0,3},{1,2},{2,1},{3,0},{4,7},{5,6},{6,5},{7,4},{8,11},{9,10},{10,... | collective-permute-start | bytes 589832 | tf_op jit(solution)/shard_map/ppermute | solution.py:558
  222.7 52.2 %collective-permute-start.30 = (bf16[768,192]{1,0:T(8,128)(2,1)}, bf16[768,192]{1,0:T(8,128)(2,1)}, u32[]{:S(2)}, u32[]{:S(2)}) collective-permute-start(bf16[768,192]{1,0:T(8,128)(2,1)} %get-tuple-element.107), channel_id=1, source_target_pairs={{0,1},{1,0},{2,3},{3,2},{4,5},{5,4},{6,7},{7,6},{8,9},{9,8},{10,11... | collective-permute-start | bytes 884744 | tf_op jit(solution)/shard_map/ppermute | solution.py:558
  223.9 51.1 %collective-permute-start.32 = (bf16[768,192]{1,0:T(8,128)(2,1)S(1)}, bf16[768,192]{1,0:T(8,128)(2,1)}, u32[]{:S(2)}, u32[]{:S(2)}) collective-permute-start(bf16[768,192]{1,0:T(8,128)(2,1)S(1)} %add_convert_fusion.3), channel_id=1, source_target_pairs={{0,2},{1,3},{2,0},{3,1},{4,6},{5,7},{6,4},{7,5},{8,10},{9,11},{10,... | collective-permute-start | bytes 884744 | tf_op jit(solution)/shard_map/ppermute | solution.py:558
  225.2 77.3 %collective-permute-start.18 = (bf16[512,768]{1,0:T(8,128)(2,1)}, bf16[512,768]{1,0:T(8,128)(2,1)S(1)}, u32[]{:S(2)}, u32[]{:S(2)}) collective-permute-start(bf16[512,768]{1,0:T(8,128)(2,1)} %get-tuple-element.83), channel_id=1, source_target_pairs={{0,1},{1,0},{2,3},{3,2},{4,5},{5,4},{6,7},{7,6},{8,9},{9,8},{10,11... | collective-permute-start | bytes 2359304 | tf_op jit(solution)/shard_map/ppermute | solution.py:558
  228.2 76.4 %collective-permute-start.20 = (bf16[512,768]{1,0:T(8,128)(2,1)S(1)}, bf16[512,768]{1,0:T(8,128)(2,1)S(1)}, u32[]{:S(2)}, u32[]{:S(2)}) collective-permute-start(bf16[512,768]{1,0:T(8,128)(2,1)S(1)} %add_convert_fusion.2), channel_id=1, source_target_pairs={{0,2},{1,3},{2,0},{3,1},{4,6},{5,7},{6,4},{7,5},{8,10},{9,11},{10,... | collective-permute-start | bytes 2359304 | tf_op jit(solution)/shard_map/ppermute | solution.py:558
  266.4 38.1 %collective-permute-start.28 = (bf16[512,768]{1,0:T(8,128)(2,1)}, bf16[512,768]{1,0:T(8,128)(2,1)}, u32[]{:S(2)}, u32[]{:S(2)}) collective-permute-start(bf16[512,768]{1,0:T(8,128)(2,1)} %get-tuple-element.102), channel_id=1, source_target_pairs={{0,1},{1,0},{2,3},{3,2},{4,5},{5,4},{6,7},{7,6},{8,9},{9,8},{10,11... | collective-permute-start | bytes 2359304 | tf_op jit(solution)/shard_map/ppermute | solution.py:558
  301.8 13.0 %collective-permute-start.38 = (bf16[96,768]{1,0:T(8,128)(2,1)}, bf16[96,768]{1,0:T(8,128)(2,1)S(1)}, u32[]{:S(2)}, u32[]{:S(2)}) collective-permute-start(bf16[96,768]{1,0:T(8,128)(2,1)} %get-tuple-element.120), channel_id=1, source_target_pairs={{0,4},{4,0},{8,12},{12,8},{16,20},{20,16},{24,28},{28,24},{1,5},{5... | collective-permute-start | bytes 442376 | tf_op jit(solution)/shard_map/ppermute | solution.py:558
  302.0 18.6 %collective-permute-start.39 = (bf16[96,768]{1,0:T(8,128)(2,1)}, bf16[96,768]{1,0:T(8,128)(2,1)}, u32[]{:S(2)}, u32[]{:S(2)}) collective-permute-start(bf16[96,768]{1,0:T(8,128)(2,1)} %get-tuple-element.121), channel_id=1, source_target_pairs={{0,8},{4,12},{8,0},{12,4},{16,24},{20,28},{24,16},{28,20},{1,9},{5... | collective-permute-start | bytes 442376 | tf_op jit(solution)/shard_map/ppermute | solution.py:558
  302.6 18.8 %collective-permute-start.40 = (bf16[96,768]{1,0:T(8,128)(2,1)}, bf16[96,768]{1,0:T(8,128)(2,1)}, u32[]{:S(2)}, u32[]{:S(2)}) collective-permute-start(bf16[96,768]{1,0:T(8,128)(2,1)} %get-tuple-element.122), channel_id=1, source_target_pairs={{0,12},{4,8},{8,4},{12,0},{16,28},{20,24},{24,20},{28,16},{1,13},{... | collective-permute-start | bytes 442376 | tf_op jit(solution)/shard_map/ppermute | solution.py:558
  304.5 19.4 %collective-permute-start.41 = (bf16[96,768]{1,0:T(8,128)(2,1)}, bf16[96,768]{1,0:T(8,128)(2,1)}, u32[]{:S(2)}, u32[]{:S(2)}) collective-permute-start(bf16[96,768]{1,0:T(8,128)(2,1)} %get-tuple-element.123), channel_id=1, source_target_pairs={{0,16},{4,20},{8,24},{12,28},{16,0},{20,4},{24,8},{28,12},{1,17},{... | collective-permute-start | bytes 442376 | tf_op jit(solution)/shard_map/ppermute | solution.py:558
  310.6 36.8 %collective-permute-start.27 = (bf16[512,768]{1,0:T(8,128)(2,1)}, bf16[512,768]{1,0:T(8,128)(2,1)S(1)}, u32[]{:S(2)}, u32[]{:S(2)}) collective-permute-start(bf16[512,768]{1,0:T(8,128)(2,1)} %get-tuple-element.98), channel_id=1, source_target_pairs={{0,1},{1,0},{2,3},{3,2},{4,5},{5,4},{6,7},{7,6},{8,9},{9,8},{10,11... | collective-permute-start | bytes 2359304 | tf_op jit(solution)/shard_map/ppermute | solution.py:558
  314.8 32.6 %collective-permute-start.29 = (bf16[512,768]{1,0:T(8,128)(2,1)S(1)}, bf16[512,768]{1,0:T(8,128)(2,1)}, u32[]{:S(2)}, u32[]{:S(2)}) collective-permute-start(bf16[512,768]{1,0:T(8,128)(2,1)S(1)} %add_convert_fusion), channel_id=1, source_target_pairs={{0,2},{1,3},{2,0},{3,1},{4,6},{5,7},{6,4},{7,5},{8,10},{9,11},{10,... | collective-permute-start | bytes 2359304 | tf_op jit(solution)/shard_map/ppermute | solution.py:558
  321.4 18.8 %collective-permute-start.43 = (bf16[96,768]{1,0:T(8,128)(2,1)}, bf16[96,768]{1,0:T(8,128)(2,1)S(1)}, u32[]{:S(2)}, u32[]{:S(2)}) collective-permute-start(bf16[96,768]{1,0:T(8,128)(2,1)} %get-tuple-element.125), channel_id=1, source_target_pairs={{0,24},{4,28},{8,16},{12,20},{16,8},{20,12},{24,0},{28,4},{1,25},{... | collective-permute-start | bytes 442376 | tf_op jit(solution)/shard_map/ppermute | solution.py:558
  323.9 20.3 %collective-permute-start.44 = (bf16[96,768]{1,0:T(8,128)(2,1)}, bf16[96,768]{1,0:T(8,128)(2,1)S(1)}, u32[]{:S(2)}, u32[]{:S(2)}) collective-permute-start(bf16[96,768]{1,0:T(8,128)(2,1)} %get-tuple-element.126), channel_id=1, source_target_pairs={{0,28},{4,24},{8,20},{12,16},{16,12},{20,8},{24,4},{28,0},{1,29},{... | collective-permute-start | bytes 442376 | tf_op jit(solution)/shard_map/ppermute | solution.py:558
  (58 other events, 496.1 us)
Sparse Core Ops, SparseCore 0:
  31.8 53.7 all-gather.1
  186.5 67.1 reduce-scatter.1
where the time goes:
time: 369 us; the launch traced here: 362 us
  Pallas kernels  141 us (38%)
  waiting for transfers between devices  113 us (31%)
  starting transfers between devices  48.2 us (13%)
  other arithmetic  25.8 us (7%)
  between operations  16.9 us (5%)
  local copies, waits for them, and re-layouts  16.4 us (4%)
    ppermute x45, waiting for transfers between devices, hop(): return lax.ppermute(value, axis, [(i, i ^ bit) for i in range(count)])  113 us
    ppermute x45, starting transfers between devices, hop(): return lax.ppermute(value, axis, [(i, i ^ bit) for i in range(count)])  48.2 us
    pallas_call x1, Pallas kernels, attend_back(): pl.pallas_call(attend_back_kernel, grid=(slots,), in_specs=[pl.BlockSpec(...  22.1 us
    pallas_call x1, Pallas kernels, attend(): pl.pallas_call(attend_kernel, grid=(slots,), in_specs=[pl.BlockSpec((leng...  17.7 us
    pallas_call x2, Pallas kernels, unproject(): pl.pallas_call(kernel, grid=(each // ROW_STEP,), in_specs=[pl.BlockSpec((...  16.1 us
    pallas_call x2, Pallas kernels, mlp(): pl.pallas_call(mlp_kernel, grid=(each // ROW_STEP,), in_specs=[block] * 4...  15.9 us
    pallas_call x1, Pallas kernels, to_slots(): pl.pallas_call(order_kernel, grid=(rows // ROW_STEP,), in_specs=[whole] *...  11.3 us
    pallas_call x1, Pallas kernels, mlp_weights(): pl.pallas_call(mlp_weights_kernel, grid=(each // ROW_STEP,), in_specs=[bl...  10.9 us
  transfers between devices with their start and end apart: 47, of which 19 were waited for; matrix products, arithmetic and copies ran while one was open for 9% of the time, Pallas kernels for 34%

commit v1 on v0

--- a/solution.py
+++ b/solution.py
@@ -584,11 +584,9 @@
     return fold_far(pieces[0], pieces[1], fold_over(pieces[2:]))
 
 
-def add_up(terms):
-    total = terms[0].astype(f32)
-    for term in terms[1:]:
-        total = total + term.astype(f32)
-    return total
+def fold_lanes(row, width):
+    short = -row.shape[1] % width
+    return jnp.sum(jnp.pad(row, ((0, 0), (0, short))).reshape(-1, width), axis=0, keepdims=True)
 
 
 def total_all(value):
@@ -638,8 +636,11 @@
     return total
 
 
-def qkv_weights_kernel(place_ref, normed_ref, dqkv_ref, w_ref, other_ref, *refs):
-    parts, gain_ref, acc = refs[:-2], refs[-2], refs[-1]
+def qkv_weights_kernel(
+    place_ref, mix_ref, normed_ref, dqkv_ref, w_ref, a_ref, b_ref, c_ref, *refs
+):
+    gain_ref, rows_ref, own_ref, down_ref, prior_ref = refs[:5]
+    parts, packed_ref, acc = refs[5:-2], refs[-2], refs[-1]
     step = pl.program_id(0)
     cols = acc.shape[1]
     part = dot(normed_ref[...], dqkv_ref[...], ((0,), (0,)))
@@ -654,42 +655,60 @@
 
     @pl.when(step == pl.num_programs(0) - 1)
     def _():
-        gain = None
+        product = None
         third = w_ref.shape[2]
         for c in range(3):
             term = acc[:, c * third : (c + 1) * third] * w_ref[c].astype(f32)
-            gain = term if gain is None else gain + term
-        gain_ref[...] = jnp.sum(gain, axis=1, keepdims=True)
+            product = term if product is None else product + term
+        sums = lax.dot_general(
+            jnp.ones((8, third), f32),
+            product,
+            (((1,), (1,)), ((), ())),
+            precision=lax.Precision.HIGHEST,
+            preferred_element_type=f32,
+        )
+        packed_ref[0:1, :] = sums[0:1, :] / gain_ref[...]
+        packed_ref[1:2, :] = jnp.sum(rows_ref[...], axis=0)
+        packed_ref[2:6, :] = jnp.sum(prior_ref[...], axis=0)
+        packed_ref[6:7, :] = jnp.sum(own_ref[...], axis=0)
+        packed_ref[7:8, :] = down_ref[...] / mix_ref[4]
         share = acc.shape[0] // len(parts)
         for k, ref in enumerate(parts):
             at = pl.multiple_of((place_ref[0] ^ k) * share, 8)
             ref[:, :cols] = acc[pl.ds(at, share), :].astype(bf16)
-            ref[:, cols:] = other_ref[pl.ds(at, share), :].astype(bf16)
-
-
-def qkv_weights(normed, dqkv, w, other, place, count):
+            here = pl.ds(at, share)
+            other = a_ref[here, :].astype(f32) + b_ref[here, :].astype(f32)
+            ref[:, cols:] = (other + c_ref[here, :].astype(f32)).astype(bf16)
+
+
+def qkv_weights(normed, dqkv, w, others, smalls, mix, place, count):
     rows, width = normed.shape
     cols = dqkv.shape[1]
-    extra = other.shape[1]
+    extra = others[0].shape[1]
     step = 2 * ROW_STEP
     share = width // count
+
+    def whole(array):
+        return pl.BlockSpec(array.shape, lambda i: (0,) * array.ndim)
+
     return pl.pallas_call(
         qkv_weights_kernel,
         grid=(rows // step,),
         in_specs=[
             pl.BlockSpec(memory_space=pltpu.SMEM),
+            pl.BlockSpec(memory_space=pltpu.SMEM),
             pl.BlockSpec((step, width), lambda i: (i, 0)),
             pl.BlockSpec((step, cols), lambda i: (i, 0)),
             pl.BlockSpec((3,) + w.shape[1:], lambda i: (0, 0, 0)),
-            pl.BlockSpec(other.shape, lambda i: (0, 0)),
-        ],
+        ]
+        + [whole(array) for array in [*others, *smalls]],
         out_specs=[pl.BlockSpec((share, cols + extra), lambda i: (0, 0))] * count
-        + [pl.BlockSpec((width, 1), lambda i: (0, 0))],
+        + [pl.BlockSpec((8, width), lambda i: (0, 0))],
         out_shape=[jax.ShapeDtypeStruct((share, cols + extra), bf16)] * count
-        + [jax.ShapeDtypeStruct((width, 1), f32)],
+        + [jax.ShapeDtypeStruct((8, width), f32)],
         scratch_shapes=[pltpu.VMEM((width, cols), f32)],
         name="wqkv",
-    )(place, normed, dqkv, w, other)
+    )(place, mix, normed, dqkv, w, *others, *smalls)
 
 
 def layer(
@@ -759,20 +778,21 @@
     grad_after, grad_low, gain_rows, own_terms, *grad_heads = mid_back(
         mix_weights, after_attn, gain_mlp, mlp_terms, grad_out, out_pieces
     )
-    grad_gain_mlp = jnp.sum(gain_rows, axis=(0, 1))
     grad_attended = exchange_tensor(grad_heads)
-    out_scattered = add_up(scatter_tensor(out_weights(grad_low, attended)))
+    out_terms = scatter_tensor(out_weights(grad_low, attended))
 
     dqkv = attend_back(qkv, first, perm_col, grad_attended, stat, cosine, sine)
     part2, part3 = unproject(dqkv, perm_row, full_qkv, own_rows, 2)
     outward = fold_over([part2, part3])
     dp_count = lax.axis_size(DP)
     small = dp_count <= 8
-    *parts, gain_partial = qkv_weights(
+    *parts, packed = qkv_weights(
         normed_slot,
         dqkv,
         full_qkv,
-        out_scattered,
+        out_terms,
+        (gain_attn[None], gain_rows, own_terms, fold_lanes(down_terms, width), prior_terms),
+        mix_weights,
         jnp.full((1,), lax.axis_index(DP) if small else 0, jnp.int32),
         dp_count if small else 1,
     )
@@ -785,29 +805,24 @@
         grad_both = scatter_dp(parts[0])
     grad_qkv = grad_both[:, : 3 * head_cols]
     grad_out_t = grad_both[:, 3 * head_cols :]
-    grad_gain_attn = gain_partial[:, 0] / gain_attn
 
     grad_hidden = last_back(hidden_in, gain_attn, attn_terms, grad_after)
 
     mixed = mix_late(mix_weights, after_attn, mlp_total, late_prior)
-    last_term = jnp.sum(own_terms) + jnp.sum(down_terms) / mix_weights[4]
-    mix_terms = jnp.concatenate([jnp.sum(prior_terms, axis=(0, 2)), last_term[None]])
-    spare = -(2 * width + 5) % 1024
-    packed = jnp.concatenate(
-        [grad_gain_attn, grad_gain_mlp, mix_terms, jnp.zeros((spare,), f32)]
-    )
-    packed = total_all(packed.reshape(-1, LANES)).reshape(-1)
+    packed = total_all(packed)
+    lane_sums = jnp.sum(packed[2:8], axis=1)
+    grad_mix = jnp.concatenate([lane_sums[:4], lane_sums[4:5] + lane_sums[5:6]])
     return (
         mixed,
         grad_hidden,
         grad_earlier,
-        packed[:width],
-        packed[width : 2 * width],
+        packed[0],
+        packed[1],
         grad_qkv.reshape(shard_d, 3, head_cols),
         grad_out_t.T,
         grad_up,
         grad_down_t.T,
-        packed[2 * width : 2 * width + 5],
+        grad_mix,
     )
 
 

time: 369 us -> 376 us (1.019)
  the two profiles are of different devices: /device:TPU:23 before, /device:TPU:21 now
where the time goes in v1:
time: 376 us; the launch traced here: 369 us
  Pallas kernels  141 us (38%)
  waiting for transfers between devices  129 us (34%)
  starting transfers between devices  44.1 us (12%)
  other arithmetic  22.2 us (6%)
  local copies, waits for them, and re-layouts  16.5 us (4%)
  between operations  16.1 us (4%)
    ppermute x45, waiting for transfers between devices, hop(): return lax.ppermute(value, axis, [(i, i ^ bit) for i in range(count)])  129 us
    ppermute x45, starting transfers between devices, hop(): return lax.ppermute(value, axis, [(i, i ^ bit) for i in range(count)])  44 us
    pallas_call x1, Pallas kernels, attend_back(): pl.pallas_call(attend_back_kernel, grid=(slots,), in_specs=[pl.BlockSpec(...  22.6 us
    pallas_call x1, Pallas kernels, attend(): pl.pallas_call(attend_kernel, grid=(slots,), in_specs=[pl.BlockSpec((leng...  17.7 us
    pallas_call x2, Pallas kernels, unproject(): pl.pallas_call(kernel, grid=(each // ROW_STEP,), in_specs=[pl.BlockSpec((...  15.9 us
    pallas_call x2, Pallas kernels, mlp(): pl.pallas_call(mlp_kernel, grid=(each // ROW_STEP,), in_specs=[block] * 4...  15.9 us
    pallas_call x1, Pallas kernels, to_slots(): pl.pallas_call(order_kernel, grid=(rows // ROW_STEP,), in_specs=[whole] *...  11.3 us
    pallas_call x1, Pallas kernels, mlp_weights(): pl.pallas_call(mlp_weights_kernel, grid=(each // ROW_STEP,), in_specs=[bl...  10.9 us
  transfers between devices with their start and end apart: 47, of which 23 were waited for; matrix products, arithmetic and copies ran while one was open for 8% of the time, Pallas kernels for 33%

profile of v1, /device:TPU:21, one launch (start us, length us, event | category | flops | bytes accessed | tf_op | source)
XLA Modules:
  0.0 369.4 jit_solution(16700402796935508888)
XLA Ops:
  11.0 6.1 %collective-permute-done.3 = bf16[4,96,192]{2,1,0:T(8,128)(2,1)S(1)} collective-permute-done((bf16[4,96,192]{2,1,0:T(8,128)(2,1)S(1)}, bf16[4,96,192]{2,1,0:T(8,128)(2,1)S(1)}, u32[]{:S(2)}, u32[]{:S(2)}) %collective-permute-start.3) | collective-permute-done | bytes 147488 | tf_op jit(solution)/shard_map/ppermute | solution.py:558
  17.2 5.3 %collective-permute-start.4 = (bf16[4,2,96,192]{3,2,1,0:T(8,128)(2,1)S(1)}, bf16[4,2,96,192]{3,2,1,0:T(8,128)(2,1)S(1)}, u32[]{:S(2)}, u32[]{:S(2)}) collective-permute-start(bf16[4,2,96,192]{3,2,1,0:T(8,128)(2,1)S(1)} %broadcast_select_fusion.2), channel_id=1, source_target_pairs={{0,8},{4,12},{8,0},{12,4},{16,24},{20,28},{24,16},{28,20},{1,9},{5... | collective-permute-start | bytes 884744 | tf_op jit(solution)/shard_map/ppermute | solution.py:558
  23.3 8.3 %collective-permute-done.4 = bf16[4,2,96,192]{3,2,1,0:T(8,128)(2,1)S(1)} collective-permute-done((bf16[4,2,96,192]{3,2,1,0:T(8,128)(2,1)S(1)}, bf16[4,2,96,192]{3,2,1,0:T(8,128)(2,1)S(1)}, u32[]{:S(2)}, u32[]{:S(2)}) %collective-permute-start.4) | collective-permute-done | bytes 294944 | tf_op jit(solution)/shard_map/ppermute | solution.py:558
  36.4 14.9 %collective-permute-done.1.n2 = bf16[512,768]{1,0:T(8,128)(2,1)} collective-permute-done((bf16[512,768]{1,0:T(8,128)(2,1)}, bf16[512,768]{1,0:T(8,128)(2,1)}, u32[]{:S(2)}, u32[]{:S(2)}) %collective-permute-start.1) | collective-permute-done | bytes 786464 | tf_op jit(solution)/shard_map/ppermute | solution.py:558
  56.5 3.7 %fusion.5 = (f32[2048,32]{1,0:T(8,128)S(1)}, f32[2048,32]{1,0:T(8,128)S(1)}, f32[2048,32]{1,0:T(8,128)S(1)}) fusion(f32[32]{0:T(128)S(1)} %negate_power_fusion, f32[2048]{0:T(1024)S(1)} %bitcast.37), kind=kLoop, calls=%fused_computation.20 | loop fusion | flops 131072 | bytes 794752 | tf_op jit(solution)/shard_map/neg | solution.py:45
  75.0 11.3 %order.1.normed_ref = bf16[2048,768]{1,0:T(8,128)(2,1)} custom-call(bf16[512,768]{1,0:T(8,128)(2,1)} %fusion.4.n0, bf16[512,768]{1,0:T(8,128)(2,1)} %collective-permute-done.n1, bf16[512,768]{1,0:T(8,128)(2,1)} %collective-permute-done.1.n2, bf16[512,768]{1,0:T(8,128)(2,1)} %collective-permute-done.2.n3, s32[2048,1]{1,0:T(8,128)} %copy.37.perm_ref), custom_call_target="tpu_custom_call" | custom-call | tf_op jit(solution)/shard_map/order/pallas_call | solution.py:82
  86.3 7.6 %proj.1.qkv_ref = bf16[2048,576]{1,0:T(8,128)(2,1)} custom-call(bf16[2048,768]{1,0:T(8,128)(2,1)} %order.1.normed_ref, bf16[4,768,192]{2,1,0:T(8,128)(2,1)} %bitcast_select_fusion.w_ref, f32[2048,128]{1,0:T(8,128)} %get-tuple-element.175.cos_ref, f32[2048,128]{1,0:T(8,128)} %get-tuple-element.176.sin_ref), custom_call_target="tpu_custom_call" | custom-call | tf_op jit(solution)/shard_map/proj/pallas_call | solution.py:109
  93.8 17.7 %att.1 = (bf16[512,192]{1,0:T(8,128)(2,1)}, bf16[512,192]{1,0:T(8,128)(2,1)}, bf16[512,192]{1,0:T(8,128)(2,1)}, bf16[512,192]{1,0:T(8,128)(2,1)}, f32[2,8,1024]{2,1,0:T(8,128)}) custom-call(bf16[2048,576]{1,0:T(8,128)(2,1)} %proj.1.qkv_ref, s32[2,1,1024]{2,1,0:T(1,128)} %reshape.77.first_ref, s32[1,2048]{1,0:T(1,128)} %bitcast.31), custom_call_target="tpu_custom_call" | custom-call | tf_op jit(solution)/shard_map/att/pallas_call | solution.py:431
  115.0 4.3 %collective-permute-done.7.refs_2_ = bf16[512,192]{1,0:T(8,128)(2,1)S(1)} collective-permute-done((bf16[512,192]{1,0:T(8,128)(2,1)}, bf16[512,192]{1,0:T(8,128)(2,1)S(1)}, u32[]{:S(2)}, u32[]{:S(2)}) %collective-permute-start.7) | collective-permute-done | bytes 196640 | tf_op jit(solution)/shard_map/ppermute | solution.py:558
  119.3 7.1 %collective-permute-done.8.refs_3_ = bf16[512,192]{1,0:T(8,128)(2,1)S(1)} collective-permute-done((bf16[512,192]{1,0:T(8,128)(2,1)}, bf16[512,192]{1,0:T(8,128)(2,1)S(1)}, u32[]{:S(2)}, u32[]{:S(2)}) %collective-permute-start.8) | collective-permute-done | bytes 196640 | tf_op jit(solution)/shard_map/ppermute | solution.py:558
  127.1 4.2 %proj_o.1 = (f32[512,768]{1,0:T(8,128)}, bf16[512,768]{1,0:T(8,128)(2,1)}) custom-call(bf16[512,768]{1,0:T(8,128)(2,1)} %value_ref.3, f32[1,768]{1,0:T(1,128)} %broadcast_in_dim.98.gain_ref, bf16[512,192]{1,0:T(8,128)(2,1)} %get-tuple-element.70.refs_0_, bf16[512,192]{1,0:T(8,128)(2,1)} %copy-done.13, bf16[512,192]{1,0:T(8,128)(2,1)} %copy-done.14, ...), custom_call_target="tpu_custom_call" | custom-call | tf_op jit(solution)/shard_map/proj_o/pallas_call | solution.py:218
  131.7 10.0 %collective-permute-done.16.ga_ref.refs_6_ = bf16[512,768]{1,0:T(8,128)(2,1)S(1)} collective-permute-done((bf16[512,768]{1,0:T(8,128)(2,1)S(1)}, bf16[512,768]{1,0:T(8,128)(2,1)S(1)}, u32[]{:S(2)}, u32[]{:S(2)}) %collective-permute-start.16) | collective-permute-done | bytes 786464 | tf_op jit(solution)/shard_map/ppermute | solution.py:558
  143.9 14.7 %collective-permute-done.14.a_ref.refs_2_ = bf16[512,768]{1,0:T(8,128)(2,1)S(1)} collective-permute-done((bf16[512,768]{1,0:T(8,128)(2,1)}, bf16[512,768]{1,0:T(8,128)(2,1)S(1)}, u32[]{:S(2)}, u32[]{:S(2)}) %collective-permute-start.14) | collective-permute-done | bytes 786464 | tf_op jit(solution)/shard_map/ppermute | solution.py:558
  162.0 8.0 %shard_map.196 = (bf16[512,768]{1,0:T(8,128)(2,1)}, bf16[512,768]{1,0:T(8,128)(2,1)}, bf16[512,768]{1,0:T(8,128)(2,1)}, bf16[512,768]{1,0:T(8,128)(2,1)}, bf16[5...) custom-call(bf16[512,768]{1,0:T(8,128)(2,1)} %copy-done.7, bf16[512,768]{1,0:T(8,128)(2,1)} %collective-permute-done.15.b_ref.refs_3_, ...), custom_call_target="tpu_custom_call" | custom-call | tf_op jit(solution)/shard_map/pallas_call | solution.py:304
  170.0 7.8 %shard_map.195 = (bf16[512,768]{1,0:T(8,128)(2,1)}, bf16[512,768]{1,0:T(8,128)(2,1)}, bf16[512,768]{1,0:T(8,128)(2,1)}, bf16[512,768]{1,0:T(8,128)(2,1)}, bf16[5...) custom-call(bf16[512,768]{1,0:T(8,128)(2,1)} %get-tuple-element.76.a_ref.refs_0_, ...), custom_call_target="tpu_custom_call" | custom-call | tf_op jit(solution)/shard_map/pallas_call | solution.py:304
  177.9 10.9 %wmlp.1 = (bf16[768,1536]{1,0:T(8,128)(2,1)}, f32[1,768]{1,0:T(1,128)}) custom-call(bf16[512,768]{1,0:T(8,128)(2,1)} %get-tuple-element.76.a_ref.refs_0_, bf16[512,768]{1,0:T(8,128)(2,1)} %collective-permute-done.12.b_ref.refs_1_, bf16[512,768]{1,0:T(8,128)(2,1)} %copy-done.7, bf16[512,768]{1,0:T(8,128)(2,1)} %collective-permute-done.15.b_ref.refs_3_, ...), custom_call_target="tpu_custom_call" | custom-call | tf_op jit(solution)/shard_map/wmlp/pallas_call | solution.py:366
  193.7 5.6 %mlp_out.1 = (bf16[512,768]{1,0:T(8,128)(2,1)}, bf16[512,768]{1,0:T(8,128)(2,1)}, bf16[512,768]{1,0:T(8,128)(2,1)}, bf16[512,768]{1,0:T(8,128)(2,1)}) custom-call(bf16[512,768]{1,0:T(8,128)(2,1)} %get-tuple-element.78.h0.refs_8_, bf16[512,768]{1,0:T(8,128)(2,1)} %get-tuple-element.79.h1.refs_9_, bf16[512,768]{1,0:T(8,128)(2,1)} %get-tuple-element.80.h2.refs_10_, ...), custom_call_target="tpu_custom_call" | custom-call | tf_op jit(solution)/shard_map/mlp_out/pallas_call | solution.py:325
  200.1 12.3 %collective-permute-done.23.c_ref = bf16[512,768]{1,0:T(8,128)(2,1)S(1)} collective-permute-done((bf16[512,768]{1,0:T(8,128)(2,1)}, bf16[512,768]{1,0:T(8,128)(2,1)S(1)}, u32[]{:S(2)}, u32[]{:S(2)}) %collective-permute-start.23) | collective-permute-done | bytes 786464 | tf_op jit(solution)/shard_map/ppermute | solution.py:558
  213.3 5.9 %mid_b.1 = (f32[512,768]{1,0:T(8,128)}, bf16[512,768]{1,0:T(8,128)(2,1)}, f32[2,1,768]{2,1,0:T(1,128)}, f32[2,1,768]{2,1,0:T(1,128)}, bf16[512,192]{1,0:T(8,128)...) custom-call(f32[5]{0:T(128)} %mix_ref.7, ...), custom_call_target="tpu_custom_call" | custom-call | tf_op jit(solution)/shard_map/mid_b/pallas_call | solution.py:161
  226.5 4.9 %collective-permute-done.25.d2 = bf16[512,192]{1,0:T(8,128)(2,1)} collective-permute-done((bf16[512,192]{1,0:T(8,128)(2,1)}, bf16[512,192]{1,0:T(8,128)(2,1)}, u32[]{:S(2)}, u32[]{:S(2)}) %collective-permute-start.25) | collective-permute-done | bytes 196640 | tf_op jit(solution)/shard_map/ppermute | solution.py:558
  231.3 7.3 %collective-permute-done.26.d3 = bf16[512,192]{1,0:T(8,128)(2,1)} collective-permute-done((bf16[512,192]{1,0:T(8,128)(2,1)}, bf16[512,192]{1,0:T(8,128)(2,1)}, u32[]{:S(2)}, u32[]{:S(2)}) %collective-permute-start.26) | collective-permute-done | bytes 196640 | tf_op jit(solution)/shard_map/ppermute | solution.py:558
  238.6 22.6 %att_b.1.dqkv_ref = bf16[2048,576]{1,0:T(8,128)(2,1)} custom-call(bf16[2048,576]{1,0:T(8,128)(2,1)} %proj.1.qkv_ref, s32[2,1,1024]{2,1,0:T(1,128)} %reshape.77.first_ref, s32[2048,1]{1,0:T(8,128)} %copy.37.perm_ref, bf16[512,192]{1,0:T(8,128)(2,1)} %get-tuple-element.93.d0, bf16[512,192]{1,0:T(8,128)(2,1)} %copy-done.25, ...), custom_call_target="tpu_custom_call" | custom-call | tf_op jit(solution)/shard_map/att_b/pallas_call | solution.py:492
  261.2 8.0 %shard_map.198 = (bf16[512,768]{1,0:T(8,128)(2,1)}, bf16[512,768]{1,0:T(8,128)(2,1)}) custom-call(bf16[2048,576]{1,0:T(8,128)(2,1)} %att_b.1.dqkv_ref, s32[1,2048]{1,0:T(1,128)} %bitcast.32, bf16[4,768,192]{2,1,0:T(8,128)(2,1)} %bitcast_select_fusion.w_ref), custom_call_target="tpu_custom_call" | custom-call | tf_op jit(solution)/shard_map/pallas_call | solution.py:543
  272.6 4.4 %mix_e.1 = (bf16[4,512,768]{2,1,0:T(8,128)(2,1)}, f32[512,768]{1,0:T(8,128)}, f32[2,4,768]{2,1,0:T(4,128)}) custom-call(f32[5]{0:T(128)} %mix_ref.7, bf16[4,512,768]{2,1,0:T(8,128)(2,1)} %earlier_ref, bf16[512,768]{1,0:T(8,128)(2,1)} %grad_ref.2), custom_call_target="tpu_custom_call" | custom-call | tf_op jit(solution)/shard_map/mix_e/pallas_call | solution.py:250
  277.0 5.6 %collective-permute-done.32.c_ref = bf16[768,192]{1,0:T(8,128)(2,1)} collective-permute-done((bf16[768,192]{1,0:T(8,128)(2,1)}, bf16[768,192]{1,0:T(8,128)(2,1)}, u32[]{:S(2)}, u32[]{:S(2)}) %collective-permute-start.32) | collective-permute-done | bytes 294944 | tf_op jit(solution)/shard_map/ppermute | solution.py:558
  282.6 8.6 %wqkv.1 = (bf16[96,768]{1,0:T(8,128)(2,1)}, bf16[96,768]{1,0:T(8,128)(2,1)}, bf16[96,768]{1,0:T(8,128)(2,1)}, bf16[96,768]{1,0:T(8,128)(2,1)}, bf16[96,768]{1,0:...) custom-call(s32[1]{0:T(128)} %bitcast.10.place_ref, ...), custom_call_target="tpu_custom_call" | custom-call | tf_op jit(solution)/shard_map/wqkv/pallas_call | solution.py:694
  302.0 8.0 %shard_map.197 = (bf16[512,768]{1,0:T(8,128)(2,1)}, bf16[512,768]{1,0:T(8,128)(2,1)}) custom-call(bf16[2048,576]{1,0:T(8,128)(2,1)} %att_b.1.dqkv_ref, s32[1,2048]{1,0:T(1,128)} %bitcast.33, bf16[4,768,192]{2,1,0:T(8,128)(2,1)} %bitcast_select_fusion.w_ref), custom_call_target="tpu_custom_call" | custom-call | tf_op jit(solution)/shard_map/pallas_call | solution.py:543
  310.0 3.8 %collective-permute-start.27 = (bf16[512,768]{1,0:T(8,128)(2,1)}, bf16[512,768]{1,0:T(8,128)(2,1)}, u32[]{:S(2)}, u32[]{:S(2)}) collective-permute-start(bf16[512,768]{1,0:T(8,128)(2,1)} %get-tuple-element.98), channel_id=1, source_target_pairs={{0,1},{1,0},{2,3},{3,2},{4,5},{5,4},{6,7},{7,6},{8,9},{9,8},{10,11... | collective-permute-start | bytes 2359304 | tf_op jit(solution)/shard_map/ppermute | solution.py:558
  334.0 9.1 %collective-permute-done.42 = bf16[96,768]{1,0:T(8,128)(2,1)S(1)} collective-permute-done((bf16[96,768]{1,0:T(8,128)(2,1)S(1)}, bf16[96,768]{1,0:T(8,128)(2,1)S(1)}, u32[]{:S(2)}, u32[]{:S(2)}) %collective-permute-start.42) | collective-permute-done | bytes 147488 | tf_op jit(solution)/shard_map/ppermute | solution.py:558
  343.1 5.8 %collective-permute-done.43 = bf16[96,768]{1,0:T(8,128)(2,1)S(1)} collective-permute-done((bf16[96,768]{1,0:T(8,128)(2,1)S(1)}, bf16[96,768]{1,0:T(8,128)(2,1)S(1)}, u32[]{:S(2)}, u32[]{:S(2)}) %collective-permute-start.43) | collective-permute-done | bytes 147488 | tf_op jit(solution)/shard_map/ppermute | solution.py:558
  348.9 4.2 %collective-permute-done.44 = bf16[96,768]{1,0:T(8,128)(2,1)S(1)} collective-permute-done((bf16[96,768]{1,0:T(8,128)(2,1)S(1)}, bf16[96,768]{1,0:T(8,128)(2,1)S(1)}, u32[]{:S(2)}, u32[]{:S(2)}) %collective-permute-start.44) | collective-permute-done | bytes 147488 | tf_op jit(solution)/shard_map/ppermute | solution.py:558
  356.0 3.7 %last_b.1 = bf16[512,768]{1,0:T(8,128)(2,1)} custom-call(bf16[512,768]{1,0:T(8,128)(2,1)} %value_ref.3, f32[1,768]{1,0:T(1,128)} %broadcast_in_dim.111.gain_ref.refs_0_, bf16[512,768]{1,0:T(8,128)(2,1)} %get-tuple-element.100.a_ref, bf16[512,768]{1,0:T(8,128)(2,1)} %collective-permute-done.27.b_ref, bf16[512,768]{1,0:T(8,128)(2,1)} %copy-done.23, ...), custom_call_target="tpu_custom_call" | custom-call | tf_op jit(solution)/shard_map/last_b/pallas_call | solution.py:195
  (220 shorter events, 91.7 us)
Async XLA Ops:
  7.2 154.7 %all-gather.2.cloned.1.call-start = ((), (), s32[]{:S(2)}) async-start(), calls=%async_computation.1 | async-start | bytes 2654208 | tf_op jit(solution)/shard_map/all_gather | solution.py:602
  17.2 14.3 %collective-permute-start.4 = (bf16[4,2,96,192]{3,2,1,0:T(8,128)(2,1)S(1)}, bf16[4,2,96,192]{3,2,1,0:T(8,128)(2,1)S(1)}, u32[]{:S(2)}, u32[]{:S(2)}) collective-permute-start(bf16[4,2,96,192]{3,2,1,0:T(8,128)(2,1)S(1)} %broadcast_select_fusion.2), channel_id=1, source_target_pairs={{0,8},{4,12},{8,0},{12,4},{16,24},{20,28},{24,16},{28,20},{1,9},{5... | collective-permute-start | bytes 884744 | tf_op jit(solution)/shard_map/ppermute | solution.py:558
  31.7 328.1 %reduce-scatter.2.cloned.1.call-start = ((), (), s32[]{:S(2)}) async-start(), calls=%async_computation.2 | async-start | bytes 2654208 | tf_op jit(solution)/shard_map/reduce_scatter | solution.py:606
  32.9 18.3 %collective-permute-start.1 = (bf16[512,768]{1,0:T(8,128)(2,1)}, bf16[512,768]{1,0:T(8,128)(2,1)}, u32[]{:S(2)}, u32[]{:S(2)}) collective-permute-start(bf16[512,768]{1,0:T(8,128)(2,1)} %fusion.4.n0), channel_id=1, source_target_pairs={{0,2},{1,3},{2,0},{3,1},{4,6},{5,7},{6,4},{7,5},{8,10},{9,11},{10,... | collective-permute-start | bytes 2359304 | tf_op jit(solution)/shard_map/ppermute | solution.py:558
  34.1 20.9 %collective-permute-start.5 = (bf16[4,2,2,96,192]{4,3,2,1,0:T(8,128)(2,1)S(1)}, bf16[4,2,2,96,192]{4,3,2,1,0:T(8,128)(2,1)S(1)}, u32[]{:S(2)}, u32[]{:S(2)}) collective-permute-start(bf16[4,2,2,96,192]{4,3,2,1,0:T(8,128)(2,1)S(1)} %broadcast_select_fusion), channel_id=1, source_target_pairs={{0,4},{4,0},{8,12},{12,8},{16,20},{20,16},{24,28},{28,24},{1,5},{5... | collective-permute-start | bytes 1769480 | tf_op jit(solution)/shard_map/ppermute | solution.py:558
  34.4 40.6 %collective-permute-start = (bf16[512,768]{1,0:T(8,128)(2,1)}, bf16[512,768]{1,0:T(8,128)(2,1)}, u32[]{:S(2)}, u32[]{:S(2)}) collective-permute-start(bf16[512,768]{1,0:T(8,128)(2,1)} %fusion.4.n0), channel_id=1, source_target_pairs={{0,1},{1,0},{2,3},{3,2},{4,5},{5,4},{6,7},{7,6},{8,9},{9,8},{10,11... | collective-permute-start | bytes 2359304 | tf_op jit(solution)/shard_map/ppermute | solution.py:558
  51.3 23.7 %collective-permute-start.2 = (bf16[512,768]{1,0:T(8,128)(2,1)}, bf16[512,768]{1,0:T(8,128)(2,1)}, u32[]{:S(2)}, u32[]{:S(2)}) collective-permute-start(bf16[512,768]{1,0:T(8,128)(2,1)} %collective-permute-done.1.n2), channel_id=1, source_target_pairs={{0,1},{1,0},{2,3},{3,2},{4,5},{5,4},{6,7},{7,6},{8,9},{9,8},{10,11... | collective-permute-start | bytes 2359304 | tf_op jit(solution)/shard_map/ppermute | solution.py:558
  56.1 9.6 %collective-permute-start.10 = (bf16[768,192]{1,0:T(8,128)(2,1)S(1)}, bf16[768,192]{1,0:T(8,128)(2,1)}, u32[]{:S(2)}, u32[]{:S(2)}) collective-permute-start(bf16[768,192]{1,0:T(8,128)(2,1)S(1)} %bitcast.25), channel_id=1, source_target_pairs={{0,2},{1,3},{2,0},{3,1},{4,6},{5,7},{6,4},{7,5},{8,10},{9,11},{10,... | collective-permute-start | bytes 884744 | tf_op jit(solution)/shard_map/ppermute | solution.py:558
  63.3 51.7 %collective-permute-start.9 = (bf16[768,192]{1,0:T(8,128)(2,1)S(1)}, bf16[768,192]{1,0:T(8,128)(2,1)S(1)}, u32[]{:S(2)}, u32[]{:S(2)}) collective-permute-start(bf16[768,192]{1,0:T(8,128)(2,1)S(1)} %bitcast.26), channel_id=1, source_target_pairs={{0,1},{1,0},{2,3},{3,2},{4,5},{5,4},{6,7},{7,6},{8,9},{9,8},{10,11... | collective-permute-start | bytes 884744 | tf_op jit(solution)/shard_map/ppermute | solution.py:558
  65.7 49.3 %collective-permute-start.11 = (bf16[768,192]{1,0:T(8,128)(2,1)}, bf16[768,192]{1,0:T(8,128)(2,1)S(1)}, u32[]{:S(2)}, u32[]{:S(2)}) collective-permute-start(bf16[768,192]{1,0:T(8,128)(2,1)} %collective-permute-done.10.refs_6_.refs_2_), channel_id=1, source_target_pairs={{0,1},{1,0},{2,3},{3,2},{4,5},{5,4},{6,7},{7,6},{8,9},{9,8},{10,11... | collective-permute-start | bytes 884744 | tf_op jit(solution)/shard_map/ppermute | solution.py:558
  112.0 14.4 %collective-permute-start.8 = (bf16[512,192]{1,0:T(8,128)(2,1)}, bf16[512,192]{1,0:T(8,128)(2,1)S(1)}, u32[]{:S(2)}, u32[]{:S(2)}) collective-permute-start(bf16[512,192]{1,0:T(8,128)(2,1)} %get-tuple-element.74), channel_id=1, source_target_pairs={{0,3},{1,2},{2,1},{3,0},{4,7},{5,6},{6,5},{7,4},{8,11},{9,10},{10,... | collective-permute-start | bytes 589832 | tf_op jit(solution)/shard_map/ppermute | solution.py:558
  114.5 27.2 %collective-permute-start.16 = (bf16[512,768]{1,0:T(8,128)(2,1)S(1)}, bf16[512,768]{1,0:T(8,128)(2,1)S(1)}, u32[]{:S(2)}, u32[]{:S(2)}) collective-permute-start(bf16[512,768]{1,0:T(8,128)(2,1)S(1)} %multiply_convert_fusion.ga_ref.refs_4_), channel_id=1, source_target_pairs={{0,2},{1,3},{2,0},{3,1},{4,6},{5,7},{6,4},{7,5},{8,10},{9,11},{10,... | collective-permute-start | bytes 2359304 | tf_op jit(solution)/shard_map/ppermute | solution.py:558
  131.4 27.2 %collective-permute-start.14 = (bf16[512,768]{1,0:T(8,128)(2,1)}, bf16[512,768]{1,0:T(8,128)(2,1)S(1)}, u32[]{:S(2)}, u32[]{:S(2)}) collective-permute-start(bf16[512,768]{1,0:T(8,128)(2,1)} %get-tuple-element.76.a_ref.refs_0_), channel_id=1, source_target_pairs={{0,2},{1,3},{2,0},{3,1},{4,6},{5,7},{6,4},{7,5},{8,10},{9,11},{10,... | collective-permute-start | bytes 2359304 | tf_op jit(solution)/shard_map/ppermute | solution.py:558
  141.8 18.7 %collective-permute-start.17 = (bf16[512,768]{1,0:T(8,128)(2,1)S(1)}, bf16[512,768]{1,0:T(8,128)(2,1)S(1)}, u32[]{:S(2)}, u32[]{:S(2)}) collective-permute-start(bf16[512,768]{1,0:T(8,128)(2,1)S(1)} %collective-permute-done.16.ga_ref.refs_6_), channel_id=1, source_target_pairs={{0,1},{1,0},{2,3},{3,2},{4,5},{5,4},{6,7},{7,6},{8,9},{9,8},{10,11... | collective-permute-start | bytes 2359304 | tf_op jit(solution)/shard_map/ppermute | solution.py:558
  159.9 10.1 %collective-permute-start.13 = (bf16[512,768]{1,0:T(8,128)(2,1)S(1)}, bf16[512,768]{1,0:T(8,128)(2,1)}, u32[]{:S(2)}, u32[]{:S(2)}) collective-permute-start(bf16[512,768]{1,0:T(8,128)(2,1)S(1)} %multiply_convert_fusion.ga_ref.refs_4_), channel_id=1, source_target_pairs={{0,1},{1,0},{2,3},{3,2},{4,5},{5,4},{6,7},{7,6},{8,9},{9,8},{10,11... | collective-permute-start | bytes 2359304 | tf_op jit(solution)/shard_map/ppermute | solution.py:558
  160.0 10.0 %collective-permute-start.12 = (bf16[512,768]{1,0:T(8,128)(2,1)}, bf16[512,768]{1,0:T(8,128)(2,1)}, u32[]{:S(2)}, u32[]{:S(2)}) collective-permute-start(bf16[512,768]{1,0:T(8,128)(2,1)} %get-tuple-element.76.a_ref.refs_0_), channel_id=1, source_target_pairs={{0,1},{1,0},{2,3},{3,2},{4,5},{5,4},{6,7},{7,6},{8,9},{9,8},{10,11... | collective-permute-start | bytes 2359304 | tf_op jit(solution)/shard_map/ppermute | solution.py:558
  190.3 9.8 %collective-permute-start.21 = (bf16[512,768]{1,0:T(8,128)(2,1)}, bf16[512,768]{1,0:T(8,128)(2,1)S(1)}, u32[]{:S(2)}, u32[]{:S(2)}) collective-permute-start(bf16[512,768]{1,0:T(8,128)(2,1)} %get-tuple-element.90), channel_id=1, source_target_pairs={{0,1},{1,0},{2,3},{3,2},{4,5},{5,4},{6,7},{7,6},{8,9},{9,8},{10,11... | collective-permute-start | bytes 2359304 | tf_op jit(solution)/shard_map/ppermute | solution.py:558
  193.3 19.0 %collective-permute-start.23 = (bf16[512,768]{1,0:T(8,128)(2,1)}, bf16[512,768]{1,0:T(8,128)(2,1)S(1)}, u32[]{:S(2)}, u32[]{:S(2)}) collective-permute-start(bf16[512,768]{1,0:T(8,128)(2,1)} %add_convert_fusion.1), channel_id=1, source_target_pairs={{0,2},{1,3},{2,0},{3,1},{4,6},{5,7},{6,4},{7,5},{8,10},{9,11},{10,... | collective-permute-start | bytes 2359304 | tf_op jit(solution)/shard_map/ppermute | solution.py:558
  199.3 24.8 %collective-permute-start.19 = (bf16[512,768]{1,0:T(8,128)(2,1)}, bf16[512,768]{1,0:T(8,128)(2,1)S(1)}, u32[]{:S(2)}, u32[]{:S(2)}) collective-permute-start(bf16[512,768]{1,0:T(8,128)(2,1)} %get-tuple-element.85), channel_id=1, source_target_pairs={{0,1},{1,0},{2,3},{3,2},{4,5},{5,4},{6,7},{7,6},{8,9},{9,8},{10,11... | collective-permute-start | bytes 2359304 | tf_op jit(solution)/shard_map/ppermute | solution.py:558
  200.0 113.8 %collective-permute-start.18 = (bf16[512,768]{1,0:T(8,128)(2,1)}, bf16[512,768]{1,0:T(8,128)(2,1)S(1)}, u32[]{:S(2)}, u32[]{:S(2)}) collective-permute-start(bf16[512,768]{1,0:T(8,128)(2,1)} %get-tuple-element.83), channel_id=1, source_target_pairs={{0,1},{1,0},{2,3},{3,2},{4,5},{5,4},{6,7},{7,6},{8,9},{9,8},{10,11... | collective-permute-start | bytes 2359304 | tf_op jit(solution)/shard_map/ppermute | solution.py:558
  222.5 47.1 %collective-permute-start.31 = (bf16[768,192]{1,0:T(8,128)(2,1)}, bf16[768,192]{1,0:T(8,128)(2,1)}, u32[]{:S(2)}, u32[]{:S(2)}) collective-permute-start(bf16[768,192]{1,0:T(8,128)(2,1)} %get-tuple-element.109), channel_id=1, source_target_pairs={{0,1},{1,0},{2,3},{3,2},{4,5},{5,4},{6,7},{7,6},{8,9},{9,8},{10,11... | collective-permute-start | bytes 884744 | tf_op jit(solution)/shard_map/ppermute | solution.py:558
  224.1 14.5 %collective-permute-start.26 = (bf16[512,192]{1,0:T(8,128)(2,1)}, bf16[512,192]{1,0:T(8,128)(2,1)}, u32[]{:S(2)}, u32[]{:S(2)}) collective-permute-start(bf16[512,192]{1,0:T(8,128)(2,1)} %get-tuple-element.96), channel_id=1, source_target_pairs={{0,3},{1,2},{2,1},{3,0},{4,7},{5,6},{6,5},{7,4},{8,11},{9,10},{10,... | collective-permute-start | bytes 589832 | tf_op jit(solution)/shard_map/ppermute | solution.py:558
  226.0 87.7 %collective-permute-start.20 = (bf16[512,768]{1,0:T(8,128)(2,1)S(1)}, bf16[512,768]{1,0:T(8,128)(2,1)S(1)}, u32[]{:S(2)}, u32[]{:S(2)}) collective-permute-start(bf16[512,768]{1,0:T(8,128)(2,1)S(1)} %add_convert_fusion.2), channel_id=1, source_target_pairs={{0,2},{1,3},{2,0},{3,1},{4,6},{5,7},{6,4},{7,5},{8,10},{9,11},{10,... | collective-permute-start | bytes 2359304 | tf_op jit(solution)/shard_map/ppermute | solution.py:558
  269.1 52.3 %collective-permute-start.28 = (bf16[512,768]{1,0:T(8,128)(2,1)}, bf16[512,768]{1,0:T(8,128)(2,1)S(1)}, u32[]{:S(2)}, u32[]{:S(2)}) collective-permute-start(bf16[512,768]{1,0:T(8,128)(2,1)} %get-tuple-element.102), channel_id=1, source_target_pairs={{0,1},{1,0},{2,3},{3,2},{4,5},{5,4},{6,7},{7,6},{8,9},{9,8},{10,11... | collective-permute-start | bytes 2359304 | tf_op jit(solution)/shard_map/ppermute | solution.py:558
  271.6 11.0 %collective-permute-start.32 = (bf16[768,192]{1,0:T(8,128)(2,1)}, bf16[768,192]{1,0:T(8,128)(2,1)}, u32[]{:S(2)}, u32[]{:S(2)}) collective-permute-start(bf16[768,192]{1,0:T(8,128)(2,1)} %add_convert_fusion.3), channel_id=1, source_target_pairs={{0,2},{1,3},{2,0},{3,1},{4,6},{5,7},{6,4},{7,5},{8,10},{9,11},{10,... | collective-permute-start | bytes 884744 | tf_op jit(solution)/shard_map/ppermute | solution.py:558
  302.0 18.0 %collective-permute-start.37 = (f32[8,768]{1,0:T(8,128)S(1)}, f32[8,768]{1,0:T(8,128)S(1)}, u32[]{:S(2)}, u32[]{:S(2)}) collective-permute-start(f32[8,768]{1,0:T(8,128)S(1)} %add.85), channel_id=1, source_target_pairs={{0,16},{4,20},{8,24},{12,28},{16,0},{20,4},{24,8},{28,12},{1,17},{... | collective-permute-start | bytes 73736 | tf_op jit(solution)/shard_map/ppermute | solution.py:558
  310.0 45.2 %collective-permute-start.27 = (bf16[512,768]{1,0:T(8,128)(2,1)}, bf16[512,768]{1,0:T(8,128)(2,1)}, u32[]{:S(2)}, u32[]{:S(2)}) collective-permute-start(bf16[512,768]{1,0:T(8,128)(2,1)} %get-tuple-element.98), channel_id=1, source_target_pairs={{0,1},{1,0},{2,3},{3,2},{4,5},{5,4},{6,7},{7,6},{8,9},{9,8},{10,11... | collective-permute-start | bytes 2359304 | tf_op jit(solution)/shard_map/ppermute | solution.py:558
  321.4 11.3 %collective-permute-start.41 = (bf16[96,768]{1,0:T(8,128)(2,1)S(1)}, bf16[96,768]{1,0:T(8,128)(2,1)S(1)}, u32[]{:S(2)}, u32[]{:S(2)}) collective-permute-start(bf16[96,768]{1,0:T(8,128)(2,1)S(1)} %copy-done.40), channel_id=1, source_target_pairs={{0,16},{4,20},{8,24},{12,28},{16,0},{20,4},{24,8},{28,12},{1,17},{... | collective-permute-start | bytes 442376 | tf_op jit(solution)/shard_map/ppermute | solution.py:558
  325.2 29.9 %collective-permute-start.29 = (bf16[512,768]{1,0:T(8,128)(2,1)}, bf16[512,768]{1,0:T(8,128)(2,1)S(1)}, u32[]{:S(2)}, u32[]{:S(2)}) collective-permute-start(bf16[512,768]{1,0:T(8,128)(2,1)} %add_convert_fusion), channel_id=1, source_target_pairs={{0,2},{1,3},{2,0},{3,1},{4,6},{5,7},{6,4},{7,5},{8,10},{9,11},{10,... | collective-permute-start | bytes 2359304 | tf_op jit(solution)/shard_map/ppermute | solution.py:558
  327.5 15.7 %collective-permute-start.42 = (bf16[96,768]{1,0:T(8,128)(2,1)S(1)}, bf16[96,768]{1,0:T(8,128)(2,1)S(1)}, u32[]{:S(2)}, u32[]{:S(2)}) collective-permute-start(bf16[96,768]{1,0:T(8,128)(2,1)S(1)} %copy-done.39), channel_id=1, source_target_pairs={{0,20},{4,16},{8,28},{12,24},{16,4},{20,0},{24,12},{28,8},{1,21},{... | collective-permute-start | bytes 442376 | tf_op jit(solution)/shard_map/ppermute | solution.py:558
  329.4 19.5 %collective-permute-start.43 = (bf16[96,768]{1,0:T(8,128)(2,1)S(1)}, bf16[96,768]{1,0:T(8,128)(2,1)S(1)}, u32[]{:S(2)}, u32[]{:S(2)}) collective-permute-start(bf16[96,768]{1,0:T(8,128)(2,1)S(1)} %copy-done.38), channel_id=1, source_target_pairs={{0,24},{4,28},{8,16},{12,20},{16,8},{20,12},{24,0},{28,4},{1,25},{... | collective-permute-start | bytes 442376 | tf_op jit(solution)/shard_map/ppermute | solution.py:558
  332.8 20.3 %collective-permute-start.44 = (bf16[96,768]{1,0:T(8,128)(2,1)S(1)}, bf16[96,768]{1,0:T(8,128)(2,1)S(1)}, u32[]{:S(2)}, u32[]{:S(2)}) collective-permute-start(bf16[96,768]{1,0:T(8,128)(2,1)S(1)} %copy-done.37), channel_id=1, source_target_pairs={{0,28},{4,24},{8,20},{12,16},{16,12},{20,8},{24,4},{28,0},{1,29},{... | collective-permute-start | bytes 442376 | tf_op jit(solution)/shard_map/ppermute | solution.py:558
  (57 other events, 509.3 us)
Sparse Core Ops, SparseCore 0:
  31.8 53.7 all-gather.1
  189.0 66.3 reduce-scatter.1
